TPU v7x, 512 devices: a whole 4x8x8 slice. The times are simulated.
512 devices in a mesh: dp: 32 (over z, x), expert: 16 (over y, core).
Axes of the slice: x: 4, y: 8, z: 8, core: 2. Of those that a mesh axis runs over, the one named last changes fastest.
Arguments:
- tokens: bfloat16 [100352, 1024], P(('dp', 'expert')), may hold values from -6 to 6
- route_weight: bfloat16 [100352], P(('dp', 'expert')), may hold values from 0.29882812 to 1
- expert_ids: int32 [100352, 1], P(('dp', 'expert')), may hold values from 0 to 15; in each aligned block of 196 rows (0 to 195, 196 to 391, ...) at most 24 rows name the same one
- visible: int32 [2048, 49], P(('dp', 'expert')), may hold values from 0 to 195, as said below
- owner_map: int32 [2048], P(('dp', 'expert')), may hold values from 0 to 15, as said below
- norm_gain: float32 [1024], replicated, may hold values from 0.5 to 1.5
- expert_in: bfloat16 [16, 2048, 1024], P('expert', 'dp'), may hold values from -0.1875 to 0.1875
- expert_out: bfloat16 [16, 2048, 1024], P('expert', 'dp'), may hold values from -0.125 to 0.125
- final_gain: float32 [1024], replicated, may hold values from 0.5 to 1.5
- embed_weight: bfloat16 [1024, 512], replicated, may hold values from -0.1875 to 0.1875
- mask_token: bfloat16 [512], replicated, may hold values from -4 to 4
- decoder_pos: bfloat16 [196, 512], replicated, may hold values from -3 to 3
- decoder_gain: float32 [512], replicated, may hold values from 0.5 to 1.5
- attention_in: bfloat16 [512, 1536], replicated
- attention_out: bfloat16 [512, 512], replicated, may hold values from -0.25 to 0.25
Outputs:
- decoded_grid: bfloat16 [2048, 196, 512], P(('dp', 'expert'))
Inputs may be any that keep to these rules, and one draw needn't show every extreme that they name: `expert_ids`: in each aligned block of 196 rows (the tokens of one device) no expert is named by more than 24 rows. `visible`: each row names 49 different positions. `owner_map`: the 4 images of an aligned block (one device) share one owner; in each aligned block of 64 images the 16 blocks have different owners.
All inputs are finite; a program needn't handle non-finite values.
Results may differ from a plain program's by a relative error of at most 0.009.
Values may be sent and summed in bfloat16 or wider, within the bound.
A program may use at most 64 MiB of HBM per device.

v0:
```python
import jax
import jax.numpy as jnp
from jax import lax
from jax.sharding import PartitionSpec as P

D = 1024
HEADS = 16
HEAD_DIM = 32
DD = 512
GRID = 196
VIS = 49


EPSILON = 1e-06


def layer_norm(values, factor):
    values = values.astype(jnp.float32)
    centered = values - jnp.mean(values, axis=-1, keepdims=True)
    variance = jnp.mean(centered * centered, axis=-1, keepdims=True)
    return centered * lax.rsqrt(variance + EPSILON) * factor


def slot_table(token_expert, experts, capacity):
    onehot = (token_expert[:, None] == jnp.arange(experts, dtype=jnp.int32)[None, :]).astype(
        jnp.int32
    )
    earlier = jnp.sum((jnp.cumsum(onehot, axis=0) - onehot) * onehot, axis=1)
    slot_index = token_expert * capacity + earlier
    return (slot_index[:, None] == jnp.arange(experts * capacity, dtype=jnp.int32)[None, :]).astype(
        jnp.bfloat16
    )


def embed_rows(merged, final_gain, embed_weight):
    final_normed = layer_norm(merged, final_gain).astype(jnp.bfloat16)
    return jnp.dot(final_normed, embed_weight, preferred_element_type=jnp.float32).astype(
        jnp.bfloat16
    )


def per_device(
    tokens,
    route_weight,
    expert_ids,
    visible,
    owner_map,
    norm_gain,
    expert_in,
    expert_out,
    final_gain,
    embed_weight,
    mask_token,
    decoder_pos,
    decoder_gain,
    attention_in,
    attention_out,
):
    groups = lax.axis_size("expert")
    tok_dev = tokens.shape[0]
    img_dev = visible.shape[0]
    exp_dev = expert_in.shape[0]
    experts = exp_dev * groups
    capacity = 2 * tok_dev // experts
    own_index = lax.axis_index("expert")
    token_expert = expert_ids[:, 0]
    all_ids, all_visible, all_owner = (
        lax.all_gather(token_expert, "expert", axis=0, tiled=True),
        lax.all_gather(visible, "expert", axis=0, tiled=True),
        lax.all_gather(owner_map, "expert", axis=0, tiled=True),
    )
    placing = slot_table(token_expert, experts, capacity)
    send_rows = jnp.dot(placing.T, tokens, preferred_element_type=jnp.float32).astype(jnp.bfloat16)
    send_weight = jnp.einsum(
        "ts,t->s", placing, route_weight, preferred_element_type=jnp.float32
    ).astype(jnp.bfloat16)
    arrived_rows, arrived_weight = (
        lax.all_to_all(
            send_rows.reshape(groups, exp_dev * capacity, D),
            "expert",
            split_axis=0,
            concat_axis=0,
            tiled=True,
        ),
        lax.all_to_all(
            send_weight.reshape(groups, exp_dev * capacity),
            "expert",
            split_axis=0,
            concat_axis=0,
            tiled=True,
        ),
    )
    expert_rows = (
        arrived_rows.reshape(groups, exp_dev, capacity, D)
        .transpose(1, 0, 2, 3)
        .reshape(exp_dev, groups * capacity, D)
    )
    expert_weight = (
        arrived_weight.reshape(groups, exp_dev, capacity)
        .transpose(1, 0, 2)
        .reshape(exp_dev, groups * capacity)
    )
    normed = layer_norm(expert_rows, norm_gain).astype(jnp.bfloat16)
    piece_in = lax.all_gather(expert_in, "dp", axis=1, tiled=True)
    piece_out = lax.all_gather(expert_out, "dp", axis=1, tiled=True)
    hidden = jax.nn.gelu(
        jnp.einsum("esd,efd->esf", normed, piece_in, preferred_element_type=jnp.float32)
    ).astype(jnp.bfloat16)
    update = jnp.einsum("esf,efd->esd", hidden, piece_out, preferred_element_type=jnp.float32)
    merged = (
        expert_rows.astype(jnp.float32) + expert_weight.astype(jnp.float32)[:, :, None] * update
    ).astype(jnp.bfloat16)
    source_owner = all_owner.reshape(groups, img_dev)[:, 0]
    to_owner = (source_owner[None, :] == jnp.arange(groups, dtype=jnp.int32)[:, None]).astype(
        jnp.bfloat16
    )
    source = jnp.sum(
        jnp.arange(groups, dtype=jnp.int32) * (source_owner == own_index).astype(jnp.int32)
    )
    source_ids = lax.dynamic_slice_in_dim(all_ids, source * tok_dev, tok_dev)
    source_visible = lax.dynamic_slice_in_dim(all_visible, source * img_dev, img_dev)
    source_table = slot_table(source_ids, experts, capacity)
    payload = (
        merged.reshape(exp_dev, groups, capacity, D)
        .transpose(1, 0, 2, 3)
        .reshape(groups, exp_dev * capacity, D)
    )
    outgoing = jnp.einsum(
        "os,scw->ocw", to_owner, payload, preferred_element_type=jnp.float32
    ).astype(jnp.bfloat16)
    arrived = lax.all_to_all(outgoing, "expert", split_axis=0, concat_axis=0, tiled=True)
    own_rows = jnp.dot(
        source_table, arrived.reshape(experts * capacity, D), preferred_element_type=jnp.float32
    ).astype(jnp.bfloat16)
    embedded = embed_rows(own_rows, final_gain, embed_weight)
    image_rows = embedded.reshape(img_dev, 1, VIS, DD)
    image_places = source_visible.reshape(img_dev, 1, VIS)

    def decode_image(operands):
        rows_one, places_one = operands
        position_hit = places_one[:, :, None] == jnp.arange(GRID, dtype=jnp.int32)[None, None, :]
        covered = jnp.any(position_hit, axis=1)
        placed = jnp.einsum(
            "ivg,ivd->igd",
            position_hit.astype(jnp.bfloat16),
            rows_one,
            preferred_element_type=jnp.float32,
        )
        canvas = jnp.where(
            covered[:, :, None], placed, mask_token.astype(jnp.float32)[None, None, :]
        )
        initial = canvas + decoder_pos.astype(jnp.float32)[None]
        dec_normed = layer_norm(initial, decoder_gain).astype(jnp.bfloat16)
        projected = jnp.dot(
            dec_normed.reshape(GRID, DD), attention_in, preferred_element_type=jnp.float32
        ).astype(jnp.bfloat16)
        projected = projected.reshape(1, GRID, 3, HEADS, HEAD_DIM)
        queries = projected[:, :, 0]
        key_rows = projected[:, :, 1]
        value_rows = projected[:, :, 2]
        scores = jnp.einsum(
            "iqhc,ikhc->ihqk", queries, key_rows, preferred_element_type=jnp.float32
        ) * HEAD_DIM ** (-0.5)
        highest = jnp.max(scores, axis=-1, keepdims=True)
        raised = jnp.exp(scores - highest)
        weights = (raised / jnp.sum(raised, axis=-1, keepdims=True)).astype(jnp.bfloat16)
        mixed = jnp.einsum(
            "ihqk,ikhc->iqhc", weights, value_rows, preferred_element_type=jnp.float32
        ).astype(jnp.bfloat16)
        update_out = jnp.dot(
            mixed.reshape(GRID, DD), attention_out, preferred_element_type=jnp.float32
        )
        return (initial + update_out.reshape(1, GRID, DD)).astype(jnp.bfloat16)

    decoded = lax.map(decode_image, (image_rows, image_places))
    return decoded.reshape(img_dev, GRID, DD)


def solution(mesh):
    return jax.shard_map(
        per_device,
        mesh=mesh,
        in_specs=(
            P(("dp", "expert"), None),
            P(("dp", "expert")),
            P(("dp", "expert"), None),
            P(("dp", "expert"), None),
            P(("dp", "expert")),
            P(),
            P("expert", "dp", None),
            P("expert", "dp", None),
            P(),
            P(),
            P(),
            P(),
            P(),
            P(),
            P(),
        ),
        out_specs=P(("dp", "expert"), None, None),
        check_vma=False,
    )
```

profile of v0, /device:TPU:1, one launch (start us, length us, event | category | flops | bytes accessed | tf_op | source)
XLA Modules:
  0.0 293.3 jit_solution(7976622157471527330)
XLA Ops:
  6.5 0.7 all-gather.5.cloned.1.call-update
  7.3 0.7 all-gather.7.cloned.1.call-update
  8.0 0.7 iota_compare_fusion.7
  8.7 0.6 reduce-window.16
  9.5 0.7 reshape.439
  10.3 0.7 fusion.56
  11.0 0.7 multiply_add_fusion
  11.9 0.7 all_to_all.16
  12.6 10.1 %all-to-all-start.1 = ((bf16[16,1,24]{2,1,0:T(2,128)(2,1)}), bf16[16,1,24]{2,1,0:T(2,128)(2,1)S(1)}, u32[]{:S(2)}, u32[]{:S(2)}) async-start(bf16[16,1,24]{2,1,0:T(2,128)(2,1)} %all_to_all.16), calls=%async_computation.1 | async-start | bytes 16384 | tf_op jit(solution)/shard_map/all_to_all | solution.py:85
  22.6 2.4 convolution_convert_fusion.2
  25.0 4.7 %all-to-all-done.1 = bf16[16,1,24]{2,1,0:T(2,128)(2,1)S(1)} async-done(((bf16[16,1,24]{2,1,0:T(2,128)(2,1)}), bf16[16,1,24]{2,1,0:T(2,128)(2,1)S(1)}, u32[]{:S(2)}, u32[]{:S(2)}) %all-to-all-start.1) | async-done | bytes 800 | tf_op jit(solution)/shard_map/all_to_all | solution.py:85
  29.7 4.2 %all-to-all-start = ((bf16[16,24,1024]{2,1,0:T(8,128)(2,1)}), bf16[16,24,1024]{2,1,0:T(8,128)(2,1)S(1)}, u32[]{:S(2)}, u32[]{:S(2)}) async-start(bf16[16,24,1024]{2,1,0:T(8,128)(2,1)} %bitcast.22), calls=%async_computation | async-start | bytes 1572864 | tf_op jit(solution)/shard_map/all_to_all | solution.py:78
  33.9 1.3 dynamic-slice.1
  36.9 55.7 %all-reduce.4 = (s32[64]{0:T(128)S(1)}, s32[3136]{0:T(1024)S(1)}) all-reduce(s32[64]{0:T(128)S(1)} %dynamic-update-slice, s32[3136]{0:T(1024)S(1)} %dynamic-update-slice.1), channel_id=1, replica_groups=mesh['dp'=32,'expert'=16] {'expert'}, use_global_device_ids=true, to_apply=%add.2 | all-reduce | flops 3200 | bytes 25600
  94.1 7.1 %all-gather.5.cloned.1.call-done = bf16[1,2048,1024]{2,1,0:T(8,128)(2,1)} async-done(((bf16[1,64,1024]{2,1,0:T(8,128)(2,1)}), bf16[1,2048,1024]{2,1,0:T(8,128)(2,1)}) %all-gather.5.cloned.1.call-update) | async-done | bytes 4194320 | tf_op jit(solution)/shard_map/all_gather | solution.py:104
  101.2 88.0 %all-gather.7.cloned.1.call-done = bf16[1,2048,1024]{2,1,0:T(8,128)(2,1)} async-done(((bf16[1,64,1024]{2,1,0:T(8,128)(2,1)}), bf16[1,2048,1024]{2,1,0:T(8,128)(2,1)}) %all-gather.7.cloned.1.call-update) | async-done | bytes 4194320 | tf_op jit(solution)/shard_map/all_gather | solution.py:105
  189.2 7.1 %fusion.42 = bf16[384,1024]{1,0:T(8,128)(2,1)S(1)} fusion(bf16[1,2048,1024]{2,1,0:T(8,128)(2,1)} %all-gather.7.cloned.1.call-done, bf16[384,1024]{1,0:T(8,128)(2,1)S(1)} %bitcast.150, bf16[1,2048,1024]{2,1,0:T(8,128)(2,1)} %all-gather.5.cloned.1.call-done, bf16[16,24,1024]{2,1,0:T(8,128)(2,1)S(1)} %all-to-all-done, f32[384]{0:T(512)S(1)} %reshape.421), kind=kOutput, calls=%fused_computation.55 | convolution fusion | flops 3229876224 | bytes 10749440 | tf_op jit(solution)/shard_map/esf,efd->esd/dot_general | solution.py:109
  196.3 0.6 convolution_convert_fusion.1
  197.0 1.3 copy.52
  198.3 10.9 %all-to-all-start.2 = ((bf16[16,24,1024]{2,1,0:T(8,128)(2,1)}), bf16[16,24,1024]{2,1,0:T(8,128)(2,1)S(1)}, u32[]{:S(2)}, u32[]{:S(2)}) async-start(bf16[16,24,1024]{2,1,0:T(8,128)(2,1)} %copy.52), calls=%async_computation.2 | async-start | bytes 1572864 | tf_op jit(solution)/shard_map/all_to_all | solution.py:131
  209.3 0.7 fusion.62
  210.8 0.6 reduce-window.14
  212.3 28.1 %all-gather.1 = s32[16,4,49]{2,1,0:T(4,128)S(1)} all-gather(s32[1,4,49]{2,1,0:T(4,128)S(1)} %bitcast.159), channel_id=1, replica_groups=mesh['dp'=32,'expert'=16] {'expert'}, dimensions={0}, use_global_device_ids=true | all-gather | bytes 13328 | tf_op jit(solution)/shard_map/all_gather | solution.py:69
  240.6 0.5 fusion.69
  241.4 0.5 convolution_convert_fusion.4
  241.9 0.8 reshape.416
  242.6 41.3 %while.10 = (s32[]{:T(128)}, bf16[4,1,196,512]{3,2,1,0:T(8,128)(2,1)}, s32[4,1,49]{2,1,0:T(1,128)S(1)}, bf16[4,1,49,512]{3,2,1,0:T(8,128)(2,1)}, bf16[512]{0:T(5...) while((s32[]{:T(128)}, ...), condition=%wide.region_17.18_spmd, body=%wide.region_11.17_spmd.sunk | while | flops 504361024 | bytes 12126609 | solution.py:175
  242.8 1.4 fusion.92
  244.4 1.9 convolution_convert_fusion.6
  246.6 3.0 %fusion.93 = (f32[16,196]{1,0:T(8,128)S(1)}, f32[16,196,196]{1,2,0:T(8,128)}) fusion(bf16[1,196,3,16,32]{1,4,3,2,0:T(8,128)(2,1)S(1)} %bitcast.145), kind=kOutput, calls=%fused_computation.115.clone.1 | convolution fusion | flops 41182148 | bytes 2995456 | tf_op jit(solution)/shard_map/while/body/eval_jaxpr/sub | solution.py:165
  249.6 2.4 fusion.94
  252.0 1.0 fusion.95
  253.1 1.4 fusion.92
  254.7 1.9 convolution_convert_fusion.6
  256.9 3.0 %fusion.93 = (f32[16,196]{1,0:T(8,128)S(1)}, f32[16,196,196]{1,2,0:T(8,128)}) fusion(bf16[1,196,3,16,32]{1,4,3,2,0:T(8,128)(2,1)S(1)} %bitcast.145), kind=kOutput, calls=%fused_computation.115.clone.1 | convolution fusion | flops 41182148 | bytes 2995456 | tf_op jit(solution)/shard_map/while/body/eval_jaxpr/sub | solution.py:165
  259.9 2.4 fusion.94
  262.3 1.0 fusion.95
  263.4 1.4 fusion.92
  265.0 1.9 convolution_convert_fusion.6
  267.3 3.0 %fusion.93 = (f32[16,196]{1,0:T(8,128)S(1)}, f32[16,196,196]{1,2,0:T(8,128)}) fusion(bf16[1,196,3,16,32]{1,4,3,2,0:T(8,128)(2,1)S(1)} %bitcast.145), kind=kOutput, calls=%fused_computation.115.clone.1 | convolution fusion | flops 41182148 | bytes 2995456 | tf_op jit(solution)/shard_map/while/body/eval_jaxpr/sub | solution.py:165
  270.3 2.4 fusion.94
  272.7 1.0 fusion.95
  273.8 1.4 fusion.92
  275.4 1.9 convolution_convert_fusion.6
  277.6 3.0 %fusion.93 = (f32[16,196]{1,0:T(8,128)S(1)}, f32[16,196,196]{1,2,0:T(8,128)}) fusion(bf16[1,196,3,16,32]{1,4,3,2,0:T(8,128)(2,1)S(1)} %bitcast.145), kind=kOutput, calls=%fused_computation.115.clone.1 | convolution fusion | flops 41182148 | bytes 2995456 | tf_op jit(solution)/shard_map/while/body/eval_jaxpr/sub | solution.py:165
  280.6 2.4 fusion.94
  283.0 1.0 fusion.95
  284.0 2.4 copy.67
  (86 shorter events, 5.7 us)
Async XLA Ops:
  6.5 234.9 %copy-start = (bf16[1024,512]{1,0:T(8,128)(2,1)S(1)}, bf16[1024,512]{1,0:T(8,128)(2,1)}, u32[]{:S(2)}) copy-start(bf16[1024,512]{1,0:T(8,128)(2,1)} %param.26) | copy-start | bytes 3145732
  6.5 29.8 %copy-start.4 = (s32[196,1]{0,1:T(1,128)S(1)}, s32[196,1]{0,1:T(1,128)}, u32[]{:S(2)}) copy-start(s32[196,1]{0,1:T(1,128)} %param.19) | copy-start | bytes 2356
  6.5 30.1 %copy-start.8 = (s32[4]{0:T(128)S(1)}, s32[4]{0:T(128)}, u32[]{:S(2)}) copy-start(s32[4]{0:T(128)} %param.21) | copy-start | bytes 52
  6.5 94.7 %all-gather.5.cloned.1.call-start = ((), (), s32[]{:S(2)}) async-start(), calls=%async_computation.3 | async-start | bytes 4325376 | tf_op jit(solution)/shard_map/all_gather | solution.py:104
  7.3 182.0 %all-gather.7.cloned.1.call-start = ((), (), s32[]{:S(2)}) async-start(), calls=%async_computation.4 | async-start | bytes 4325376 | tf_op jit(solution)/shard_map/all_gather | solution.py:105
  12.6 17.1 %all-to-all-start.1 = ((bf16[16,1,24]{2,1,0:T(2,128)(2,1)}), bf16[16,1,24]{2,1,0:T(2,128)(2,1)S(1)}, u32[]{:S(2)}, u32[]{:S(2)}) async-start(bf16[16,1,24]{2,1,0:T(2,128)(2,1)} %all_to_all.16), calls=%async_computation.1 | async-start | bytes 16384 | tf_op jit(solution)/shard_map/all_to_all | solution.py:85
  29.7 64.0 %copy-start.5 = (f32[1024]{0:T(1024)S(1)}, f32[1024]{0:T(1024)}, u32[]{:S(2)}) copy-start(f32[1024]{0:T(1024)} %param.22) | copy-start | bytes 12292
  29.7 63.2 %all-to-all-start = ((bf16[16,24,1024]{2,1,0:T(8,128)(2,1)}), bf16[16,24,1024]{2,1,0:T(8,128)(2,1)S(1)}, u32[]{:S(2)}, u32[]{:S(2)}) async-start(bf16[16,24,1024]{2,1,0:T(8,128)(2,1)} %bitcast.22), calls=%async_computation | async-start | bytes 1572864 | tf_op jit(solution)/shard_map/all_to_all | solution.py:78
  196.3 16.0 %copy-start.7 = (s32[4,49]{1,0:T(4,128)S(1)}, s32[4,49]{1,0:T(4,128)}, u32[]{:S(2)}) copy-start(s32[4,49]{1,0:T(4,128)} %param.20) | copy-start | bytes 2356
  197.0 44.4 %copy-start.6 = (f32[1024]{0:T(1024)S(1)}, f32[1024]{0:T(1024)}, u32[]{:S(2)}) copy-start(f32[1024]{0:T(1024)} %param.25) | copy-start | bytes 12292
  198.3 44.3 %copy-start.1 = (bf16[512,512]{1,0:T(8,128)(2,1)S(1)}, bf16[512,512]{1,0:T(8,128)(2,1)}, u32[]{:S(2)}) copy-start(bf16[512,512]{1,0:T(8,128)(2,1)} %param.31) | copy-start | bytes 1572868
  198.3 44.3 %copy-start.2 = (f32[512]{0:T(512)S(1)}, f32[512]{0:T(512)}, u32[]{:S(2)}) copy-start(f32[512]{0:T(512)} %param.29) | copy-start | bytes 6148
  198.3 44.3 %copy-start.3 = (bf16[512]{0:T(512)(128)(2,1)S(1)}, bf16[512]{0:T(512)(128)(2,1)}, u32[]{:S(2)}) copy-start(bf16[512]{0:T(512)(128)(2,1)} %param.27) | copy-start | bytes 3076
  198.3 42.3 %all-to-all-start.2 = ((bf16[16,24,1024]{2,1,0:T(8,128)(2,1)}), bf16[16,24,1024]{2,1,0:T(8,128)(2,1)S(1)}, u32[]{:S(2)}, u32[]{:S(2)}) async-start(bf16[16,24,1024]{2,1,0:T(8,128)(2,1)} %copy.52), calls=%async_computation.2 | async-start | bytes 1572864 | tf_op jit(solution)/shard_map/all_to_all | solution.py:131
Sparse Core Ops, SparseCore 0:
  10.5 90.6 all-gather.4
  104.4 84.8 all-gather.6
where the time goes:
time: 294 us; the launch traced here: 293 us
  waiting for transfers between devices  101 us (34%)
  blocking collectives  83.8 us (29%)
  matrix products  50.2 us (17%)
  starting transfers between devices  25.2 us (9%)
  between operations  16.2 us (6%)
  local copies, waits for them, and re-layouts  9.71 us (3%)
  other arithmetic  6.8 us (2%)
    all_gather x1, waiting for transfers between devices, per_device(): piece_out = lax.all_gather(expert_out, 'dp', axis=1, tiled=True)  88 us
    unnamed x1, blocking collectives  55.7 us
    all_gather x1, blocking collectives, per_device(): lax.all_gather(visible, 'expert', axis=0, tiled=True)  28.1 us
    sub x4, matrix products, decode_image(): raised = jnp.exp(scores - highest)  12 us
    all_to_all x1, starting transfers between devices, per_device(): lax.all_to_all(outgoing, 'expert', split_axis=0, concat_axis=0, tiled=True)  10.9 us
    all_to_all x1, starting transfers between devices, per_device(): lax.all_to_all(send_weight.reshape(groups, exp_dev * capacity), 'expert',...  10.1 us
    dot_general x4, matrix products, decode_image(): jnp.einsum('ihqk,ikhc->iqhc', weights, value_rows, preferred_element_type...  9.58 us
    dot_general x4, matrix products, decode_image(): jnp.dot(dec_normed.reshape(GRID, DD), attention_in, preferred_element_typ...  7.77 us
  transfers between devices with their start and end apart: 5, of which 3 were waited for; matrix products, arithmetic and copies ran while one was open for 4% of the time, Pallas kernels for 0%

commit v1 on v0

v1 whole, which is shorter than its diff:
```python
import heapq

import jax
import jax.numpy as jnp
from jax import lax
from jax.experimental import pallas as pl
from jax.experimental.pallas import tpu as pltpu
from jax.sharding import PartitionSpec as P

D = 1024
HEADS = 16
HEAD_DIM = 32
DD = 512
GRID = 196
VIS = 49
TOK = 196
EXPERTS = 16
CAP = 24
SLOT = 32
ROWS = EXPERTS * SLOT
WIDE = D + 128
NX = 4
NZ = 8
UNITS = 64
PART = 48
EPSILON = 1e-06
TOKENS_AT = 20.0


def layer_norm(values, factor):
    values = values.astype(jnp.float32)
    centered = values - jnp.mean(values, axis=-1, keepdims=True)
    variance = jnp.mean(centered * centered, axis=-1, keepdims=True)
    return centered * lax.rsqrt(variance + EPSILON) * factor


def a2_max(j, way):
    return 4 if (way == 1) == (j == 0) else 3


def b1_max(way):
    return 4 if way == 1 else 3


def b2_max(k, way):
    return 2 if (way == 1) == (k % 2 == 0) else 1


def a_from(j):
    return {0: None, 1: ("a1", 0), 2: ("a1", 2), 3: ("a1", 1)}[j]


def z_step(k, longest):
    return (1, k) if k <= longest else (-1, NZ - k)


def build_plan():
    need = {("a1", 0): None, ("a1", 1): None, ("a1", 2): ("a1", 0)}
    for way in (1, -1):
        for t in range(1, b1_max(way) + 1):
            need[("b1", way, t)] = None if t == 1 else ("b1", way, t - 1)
    for k in range(NZ):
        way0, t0 = z_step(k, b1_max(1))
        for way in (1, -1):
            for t in range(1, b2_max(k, way) + 1):
                first = None if k == 0 else ("b1", way0, t0)
                need[("b2", k, way, t)] = first if t == 1 else ("b2", k, way, t - 1)
    for j in range(NX):
        for way in (1, -1):
            for t in range(1, a2_max(j, way) + 1):
                need[("a2", j, way, t)] = a_from(j) if t == 1 else ("a2", j, way, t - 1)

    def link(copy):
        if copy[0] == "a1":
            return ("x", -1 if copy[1] == 1 else 1)
        if copy[0] == "b2":
            return ("x", copy[2])
        return ("z", copy[2] if copy[0] == "a2" else copy[1])

    free = {}
    arrivals = []

    def push(copy, now):
        took = 2.1 if copy[0][0] == "a" else 3.5
        begin = max(now, free.get(link(copy), 0.0))
        free[link(copy)] = begin + took
        heapq.heappush(arrivals, (begin + took + 1.5, len(order) + len(arrivals), copy))

    order = []
    initial = [c for c in need if need[c] is None]
    for copy in initial:
        push(copy, 0.0)
    while arrivals:
        now, _, copy = heapq.heappop(arrivals)
        nexts = [c for c in need if need[c] == copy]
        order.append((now, copy, nexts))
        for c in nexts:
            push(c, now)
    slabs = []
    for k in range(NZ):
        wants = set(("b2", k, way, t) for way in (1, -1) for t in range(1, b2_max(k, way) + 1))
        if k == 0:
            wants |= {("a1", 0), ("a1", 1), ("a1", 2)}
        else:
            wants.add(("b1",) + z_step(k, b1_max(1)))
            for j in range(NX):
                wants.add(("a2", j) + z_step(k, a2_max(j, 1)))
        slabs.append(wants)
    ids = {c: i for i, c in enumerate(need)}
    return initial, order, slabs, ids


def slots_of(ids_row, rows):
    lane = ids_row.shape[1]
    expert = lax.broadcasted_iota(jnp.int32, (EXPERTS, lane), 0)
    onehot = (expert == ids_row).astype(jnp.float32)
    before = (
        lax.broadcasted_iota(jnp.int32, (lane, lane), 0)
        < lax.broadcasted_iota(jnp.int32, (lane, lane), 1)
    ).astype(jnp.bfloat16)
    count = jnp.dot(onehot.astype(jnp.bfloat16), before, preferred_element_type=jnp.float32)
    earlier = jnp.sum(count * onehot, axis=0, keepdims=True).astype(jnp.int32)
    slot = ids_row * SLOT + earlier
    return (lax.broadcasted_iota(jnp.int32, (rows, lane), 0) == slot).astype(jnp.float32)


def gelu(value):
    inner = 0.7978845608028654 * (value + 0.044715 * (value * value * value))
    return 0.5 * value * (1.0 + jnp.tanh(inner))


def expert_kernel(
    tokens_ref,
    weight_ref,
    meta_ref,
    gain_ref,
    in_ref,
    out_ref,
    final_ref,
    embed_ref,
    rows_ref,
    own_meta_ref,
    w,
    tokens_pad,
    send,
    got,
    metas,
    normed,
    total,
    outgoing,
    back,
    local_sems,
    w_send,
    w_recv,
    t_send,
    t_recv,
    m_send,
    m_recv,
    o_send,
    o_recv,
):
    initial, order, slabs, ids = build_plan()
    dp = lax.axis_index("dp")
    me = lax.axis_index("expert")
    z, x = lax.div(dp, NX), lax.rem(dp, NX)

    def at_z(step):
        return lax.rem(z + (step + NZ), NZ)

    def at_x(step):
        return lax.rem(x + (step + NX), NX)

    own_in = pltpu.make_async_copy(in_ref.at[0], w.at[z, x, pl.ds(0, UNITS)], local_sems.at[0])
    own_out = pltpu.make_async_copy(
        out_ref.at[0], w.at[z, x, pl.ds(UNITS, UNITS)], local_sems.at[1]
    )
    own_in.start()
    own_out.start()
    barrier = pltpu.get_barrier_semaphore()
    for near in (
        at_z(0) * NX + at_x(1),
        at_z(0) * NX + at_x(-1),
        at_z(1) * NX + at_x(0),
        at_z(-1) * NX + at_x(0),
    ):
        pl.semaphore_signal(
            barrier, inc=1, device_id={"dp": near}, device_id_type=pl.DeviceIdType.MESH
        )
    for d in range(1, EXPERTS):
        pl.semaphore_signal(
            barrier,
            inc=1,
            device_id={"expert": lax.rem(me + d, EXPERTS)},
            device_id_type=pl.DeviceIdType.MESH,
        )
    got[:, CAP:SLOT, :] = jnp.zeros((EXPERTS, SLOT - CAP, WIDE), jnp.bfloat16)
    back[:, CAP:SLOT, :] = jnp.zeros((EXPERTS, SLOT - CAP, DD), jnp.bfloat16)
    own_in.wait()
    own_out.wait()
    pl.semaphore_wait(barrier, 4 + EXPERTS - 1)

    def weight_copy(copy, arriving):
        kind = copy[0]
        shift = 1 if arriving else 0
        if kind == "a1":
            step = -1 if copy[1] == 1 else 1
            first = 1 if copy[1] == 2 else 0
            zi, xi = z, at_x(-step * (first + shift))
            target = at_z(0) * NX + at_x(step)
        elif kind == "b2":
            _, k, step, t = copy
            zi, xi = at_z(-k), at_x(-step * (t - 1 + shift))
            target = at_z(0) * NX + at_x(step)
        else:
            step, t = copy[-2:]
            j = copy[1] if kind == "a2" else 0
            zi, xi = at_z(-step * (t - 1 + shift)), at_x(-j)
            target = at_z(step) * NX + at_x(0)
        part = pl.ds(0, PART) if kind[0] == "a" else pl.ds(PART, 2 * UNITS - PART)
        block = w.at[zi, xi, part]
        return pltpu.make_async_remote_copy(
            src_ref=block,
            dst_ref=block,
            send_sem=w_send.at[ids[copy]],
            recv_sem=w_recv.at[ids[copy]],
            device_id={"dp": target},
            device_id_type=pl.DeviceIdType.MESH,
        )

    def exchange(src, dst, send_sem, recv_sem, d, away):
        peer = lax.rem(me + d, EXPERTS)
        from_peer = lax.rem(me + (EXPERTS - d), EXPERTS)
        return pltpu.make_async_remote_copy(
            src_ref=src(peer),
            dst_ref=dst(me if away else from_peer),
            send_sem=send_sem.at[d],
            recv_sem=recv_sem.at[d],
            device_id={"expert": peer},
            device_id_type=pl.DeviceIdType.MESH,
        )

    def meta_copy(d, away):
        return exchange(lambda p: meta_ref, lambda p: metas.at[p], m_send, m_recv, d, away)

    def token_copy(d, away):
        return exchange(
            lambda p: send.at[p, pl.ds(0, CAP)],
            lambda p: got.at[p, pl.ds(0, CAP)],
            t_send,
            t_recv,
            d,
            away,
        )

    def back_copy(d, away):
        return exchange(
            lambda p: outgoing.at[p, pl.ds(0, CAP)],
            lambda p: back.at[p, pl.ds(0, CAP)],
            o_send,
            o_recv,
            d,
            away,
        )

    for copy in initial:
        weight_copy(copy, False).start()
    for d in range(1, EXPERTS):
        meta_copy(d, True).start()
    metas[me] = meta_ref[...]

    tokens_pad[TOK // 8 * 8 :, :] = jnp.zeros((256 - TOK // 8 * 8, D), jnp.bfloat16)
    tokens_pad[0:TOK, :] = tokens_ref[...]
    placing = slots_of(meta_ref[0:1, :], ROWS)
    scale = jnp.sum(placing * weight_ref[...], axis=1, keepdims=True)
    picked = jnp.dot(
        placing.astype(jnp.bfloat16), tokens_pad[...], preferred_element_type=jnp.float32
    ).astype(jnp.bfloat16)
    send[:, :, 0:D] = picked.reshape(EXPERTS, SLOT, D)
    send[:, :, D:WIDE] = (
        jnp.broadcast_to(scale, (ROWS, 128)).astype(jnp.bfloat16).reshape(EXPERTS, SLOT, 128)
    )
    for d in range(1, EXPERTS):
        token_copy(d, True).start()
    got[me, 0:CAP, :] = send[me, 0:CAP, :]

    def begin_tokens():
        for d in range(1, EXPERTS):
            token_copy(d, False).wait_recv()
        rows = got[:, :, 0:D].reshape(ROWS, D)
        normed[...] = layer_norm(rows, gain_ref[...]).astype(jnp.bfloat16)
        total[...] = jnp.zeros((ROWS, D), jnp.float32)

    def slab(k):
        zi = at_z(-k)

        @pl.loop(0, 2)
        def _(tile):
            part = pl.ds(pl.multiple_of(tile * 256, 256), 256)
            first = w[zi, :, 0:UNITS, :].reshape(NX * UNITS, D)
            second = w[zi, :, UNITS : 2 * UNITS, :].reshape(NX * UNITS, D)
            hidden = gelu(
                lax.dot_general(
                    normed[part, :],
                    first,
                    (((1,), (1,)), ((), ())),
                    preferred_element_type=jnp.float32,
                )
            ).astype(jnp.bfloat16)
            total[part, :] += jnp.dot(hidden, second, preferred_element_type=jnp.float32)

    begun = False
    arrived = set()
    done = set()
    for now, copy, nexts in order:
        weight_copy(copy, True).wait_recv()
        for c in nexts:
            weight_copy(c, False).start()
        arrived.add(copy)
        if not begun and now > TOKENS_AT:
            begin_tokens()
            begun = True
        if begun:
            for k in range(NZ):
                if k not in done and slabs[k] <= arrived:
                    slab(k)
                    done.add(k)

    rows = got[:, :, 0:D].reshape(ROWS, D).astype(jnp.float32)
    scaling = got[:, :, D:WIDE].reshape(ROWS, 128)[:, 0:1].astype(jnp.float32)
    merged = (rows + scaling * total[...]).astype(jnp.bfloat16)
    final_normed = layer_norm(merged, final_ref[...]).astype(jnp.bfloat16)
    embedded = jnp.dot(
        final_normed, embed_ref[...], preferred_element_type=jnp.float32
    ).astype(jnp.bfloat16)
    for d in range(1, EXPERTS):
        meta_copy(d, False).wait_recv()
    owners = metas[:, 5, :][:, 0:1]
    lane = lax.broadcasted_iota(jnp.int32, (EXPERTS, ROWS), 1)
    member = lax.broadcasted_iota(jnp.int32, (EXPERTS, ROWS), 0)
    owner_lane = jnp.sum(
        jnp.where(lax.div(lane, SLOT) == member, owners, 0), axis=0, keepdims=True
    )
    row_at = lax.broadcasted_iota(jnp.int32, (ROWS, ROWS), 0)
    lane_at = lax.broadcasted_iota(jnp.int32, (ROWS, ROWS), 1)
    target_row = owner_lane * SLOT + lax.rem(lane_at[0:1, :], SLOT)
    permute = (row_at == target_row).astype(jnp.float32).astype(jnp.bfloat16)
    outgoing[...] = (
        jnp.dot(permute, embedded, preferred_element_type=jnp.float32)
        .astype(jnp.bfloat16)
        .reshape(EXPERTS, SLOT, DD)
    )
    for d in range(1, EXPERTS):
        back_copy(d, True).start()
    back[me, 0:CAP, :] = outgoing[me, 0:CAP, :]
    own_meta = jnp.zeros((8, 256), jnp.int32)
    for s in range(EXPERTS):
        entry = metas[s]
        own_meta = own_meta + jnp.where(entry[5:6, :] == me, entry, 0)
    own_meta_ref[...] = own_meta
    table = jnp.transpose(slots_of(own_meta[0:1, :], ROWS)).astype(jnp.bfloat16)
    for d in range(1, EXPERTS):
        back_copy(d, False).wait_recv()
    rows_ref[...] = jnp.dot(
        table, back[...].reshape(ROWS, DD), preferred_element_type=jnp.float32
    ).astype(jnp.bfloat16)
    for copy in ids:
        weight_copy(copy, False).wait_send()
    for d in range(1, EXPERTS):
        meta_copy(d, True).wait_send()
        token_copy(d, True).wait_send()
        back_copy(d, True).wait_send()


def expert_stage(*operands):
    vmem = pl.BlockSpec(memory_space=pltpu.VMEM)
    hbm = pl.BlockSpec(memory_space=pl.ANY)
    count = len(build_plan()[3])
    dma = pltpu.SemaphoreType.DMA
    return pl.pallas_call(
        expert_kernel,
        out_shape=(
            jax.ShapeDtypeStruct((256, DD), jnp.bfloat16),
            jax.ShapeDtypeStruct((8, 256), jnp.int32),
        ),
        in_specs=[vmem, vmem, vmem, vmem, hbm, hbm, vmem, vmem],
        out_specs=(vmem, vmem),
        scratch_shapes=[
            pltpu.VMEM((NZ, NX, 2 * UNITS, D), jnp.bfloat16),
            pltpu.VMEM((256, D), jnp.bfloat16),
            pltpu.VMEM((EXPERTS, SLOT, WIDE), jnp.bfloat16),
            pltpu.VMEM((EXPERTS, SLOT, WIDE), jnp.bfloat16),
            pltpu.VMEM((EXPERTS, 8, 256), jnp.int32),
            pltpu.VMEM((ROWS, D), jnp.bfloat16),
            pltpu.VMEM((ROWS, D), jnp.float32),
            pltpu.VMEM((EXPERTS, SLOT, DD), jnp.bfloat16),
            pltpu.VMEM((EXPERTS, SLOT, DD), jnp.bfloat16),
            dma((2,)),
            dma((count,)),
            dma((count,)),
            dma((EXPERTS,)),
            dma((EXPERTS,)),
            dma((EXPERTS,)),
            dma((EXPERTS,)),
            dma((EXPERTS,)),
            dma((EXPERTS,)),
        ],
        compiler_params=pltpu.CompilerParams(
            collective_id=0, has_side_effects=True, vmem_limit_bytes=48 * 1024 * 1024
        ),
    )(*operands)


def per_device(
    tokens,
    route_weight,
    expert_ids,
    visible,
    owner_map,
    norm_gain,
    expert_in,
    expert_out,
    final_gain,
    embed_weight,
    mask_token,
    decoder_pos,
    decoder_gain,
    attention_in,
    attention_out,
):
    img_dev = visible.shape[0]
    meta = jnp.concatenate(
        [
            jnp.pad(expert_ids.reshape(1, TOK), ((0, 0), (0, 256 - TOK)), constant_values=-1),
            jnp.pad(visible, ((0, 0), (0, 256 - VIS))),
            jnp.broadcast_to(owner_map[0], (3, 256)),
        ],
        axis=0,
    )
    weight_row = jnp.pad(
        route_weight.astype(jnp.float32).reshape(1, TOK), ((0, 0), (0, 256 - TOK))
    )
    embedded, own_meta = expert_stage(
        tokens,
        weight_row,
        meta,
        norm_gain.reshape(1, D),
        expert_in,
        expert_out,
        final_gain.reshape(1, D),
        embed_weight,
    )
    source_visible = own_meta[1:5, 0:VIS]
    image_rows = embedded[0:TOK].reshape(img_dev, 1, VIS, DD)
    image_places = source_visible.reshape(img_dev, 1, VIS)

    def decode_image(operands):
        rows_one, places_one = operands
        position_hit = places_one[:, :, None] == jnp.arange(GRID, dtype=jnp.int32)[None, None, :]
        covered = jnp.any(position_hit, axis=1)
        placed = jnp.einsum(
            "ivg,ivd->igd",
            position_hit.astype(jnp.bfloat16),
            rows_one,
            preferred_element_type=jnp.float32,
        )
        canvas = jnp.where(
            covered[:, :, None], placed, mask_token.astype(jnp.float32)[None, None, :]
        )
        initial = canvas + decoder_pos.astype(jnp.float32)[None]
        dec_normed = layer_norm(initial, decoder_gain).astype(jnp.bfloat16)
        projected = jnp.dot(
            dec_normed.reshape(GRID, DD), attention_in, preferred_element_type=jnp.float32
        ).astype(jnp.bfloat16)
        projected = projected.reshape(1, GRID, 3, HEADS, HEAD_DIM)
        queries = projected[:, :, 0]
        key_rows = projected[:, :, 1]
        value_rows = projected[:, :, 2]
        scores = jnp.einsum(
            "iqhc,ikhc->ihqk", queries, key_rows, preferred_element_type=jnp.float32
        ) * HEAD_DIM ** (-0.5)
        highest = jnp.max(scores, axis=-1, keepdims=True)
        raised = jnp.exp(scores - highest)
        weights = (raised / jnp.sum(raised, axis=-1, keepdims=True)).astype(jnp.bfloat16)
        mixed = jnp.einsum(
            "ihqk,ikhc->iqhc", weights, value_rows, preferred_element_type=jnp.float32
        ).astype(jnp.bfloat16)
        update_out = jnp.dot(
            mixed.reshape(GRID, DD), attention_out, preferred_element_type=jnp.float32
        )
        return (initial + update_out.reshape(1, GRID, DD)).astype(jnp.bfloat16)

    decoded = lax.map(decode_image, (image_rows, image_places))
    return decoded.reshape(img_dev, GRID, DD)


def solution(mesh):
    return jax.shard_map(
        per_device,
        mesh=mesh,
        in_specs=(
            P(("dp", "expert"), None),
            P(("dp", "expert")),
            P(("dp", "expert"), None),
            P(("dp", "expert"), None),
            P(("dp", "expert")),
            P(),
            P("expert", "dp", None),
            P("expert", "dp", None),
            P(),
            P(),
            P(),
            P(),
            P(),
            P(),
            P(),
        ),
        out_specs=P(("dp", "expert"), None, None),
        check_vma=False,
    )
```

time: 294 us -> 137 us (0.47)
  waiting for transfers between devices: 101 us -> 0 us
  Pallas kernels: 0 us -> 85.5 us
  blocking collectives: 83.8 us -> 0 us
  starting transfers between devices: 25.2 us -> 0 us
  between operations: 16.2 us -> 0.06 us
  matrix products: 50.2 us -> 36.3 us
    all_gather x2 -> x0, waiting for transfers between devices: 95.2 us -> none  [the longest x1 88 us: per_device(): piece_out = lax.all_gather(expert_out, 'dp', axis=1, tiled=True)]
    pallas_call x0 -> x1, Pallas kernels: none -> 85.5 us  [expert_stage(): pl.pallas_call(expert_kernel, out_shape=(jax.ShapeDtypeStruct((256, DD),...]
    unnamed x1 -> x0, blocking collectives: 55.7 us -> none
    all_gather x1 -> x0, blocking collectives: 28.1 us -> none  [per_device(): lax.all_gather(visible, 'expert', axis=0, tiled=True)]
    all_to_all x3 -> x0, starting transfers between devices: 25.2 us -> none  [the longest x1 10.9 us: per_device(): lax.all_to_all(outgoing, 'expert', split_axis=0, concat_axis=0, tiled=True)]
    dot_general x6 -> x0, matrix products: 11.3 us -> none  [the longest x1 7.08 us: per_device(): jnp.einsum('esf,efd->esd', hidden, piece_out, preferred_element_type=jnp....]
    all_to_all x3 -> x0, waiting for transfers between devices: 4.69 us -> none  [the longest x1 4.69 us: per_device(): lax.all_to_all(send_weight.reshape(groups, exp_dev * capacity), 'expert',...]
  transfers between devices with their start and end apart: 5 -> 0, of which waited for: 3 -> 0; matrix products, arithmetic and copies ran while one was open for 4% -> 0% of each run, Pallas kernels for 0% -> 0%
where the time goes in v1:
time: 137 us; the launch traced here: 136 us
  Pallas kernels  85.5 us (62%)
  matrix products  36.3 us (26%)
  local copies, waits for them, and re-layouts  9.29 us (7%)
  other arithmetic  4.74 us (3%)
    pallas_call x1, Pallas kernels, expert_stage(): pl.pallas_call(expert_kernel, out_shape=(jax.ShapeDtypeStruct((256, DD),...  85.5 us
    sub x4, matrix products, decode_image(): raised = jnp.exp(scores - highest)  12 us
    dot_general x4, matrix products, decode_image(): jnp.einsum('ihqk,ikhc->iqhc', weights, value_rows, preferred_element_type...  9.83 us
    dot_general x4, matrix products, decode_image(): jnp.dot(dec_normed.reshape(GRID, DD), attention_in, preferred_element_typ...  7.86 us
    unnamed x12, local copies, waits for them, and re-layouts  5.41 us
    dot_general x4, matrix products, decode_image(): jnp.einsum('ivg,ivd->igd', position_hit.astype(jnp.bfloat16), rows_one, p...  5.39 us

profile of v1, /device:TPU:1, one launch (start us, length us, event | category | flops | bytes accessed | tf_op | source)
XLA Modules:
  0.0 136.1 jit_solution(18363650742379191874)
XLA Ops:
  0.0 0.6 broadcast_in_dim.24
  0.7 0.8 fusion.26.meta_ref
  1.5 0.7 reshape.206
  2.2 1.2 copy-done
  3.4 1.0 copy-done.1
  4.4 0.9 copy-done.2
  5.3 0.9 copy-done.3
  6.2 0.7 copy-done.4
  6.9 0.7 copy-done.5
  7.6 85.5 %shard_map.145 = (bf16[256,512]{1,0:T(8,128)(2,1)S(1)}, s32[8,256]{1,0:T(8,128)S(1)}) custom-call(bf16[196,1024]{1,0:T(8,128)(2,1)S(1)} %copy-done.1, f32[1,256]{1,0:T(1,128)S(1)} %pad_convert_fusion.weight_ref, s32[8,256]{1,0:T(8,128)S(1)} %fusion.26.meta_ref, f32[1,1024]{1,0:T(1,128)S(1)} %bitcast.86, bf16[1,64,1024]{2,1,0:T(8,128)(2,1)S(1)} %copy-done.2, ...), custom_call_target="tpu_custom_call" | custom-call | tf_op jit(solution)/shard_map/pallas_call | solution.py:379
  93.2 41.6 %while.10 = (s32[]{:T(128)}, bf16[4,1,196,512]{3,2,1,0:T(8,128)(2,1)S(1)}, s32[4,1,49]{2,1,0:T(1,128)S(1)}, bf16[4,1,49,512]{3,2,1,0:T(8,128)(2,1)S(1)}, bf16[51...) while((s32[]{:T(128)}, ...), condition=%wide.region_6.7_spmd, body=%wide.region_0.6_spmd.sunk | while | flops 504361024 | bytes 14288941 | solution.py:492
  93.3 0.1 fusion.45
  93.4 0.7 convert_element_type.63
  94.0 1.3 fusion.46
  95.4 0.2 multiply_reduce_fusion.3
  95.6 2.0 %convolution_convert_fusion.2 = bf16[196,1536]{1,0:T(8,128)(2,1)S(1)} fusion(bf16[512,1536]{1,0:T(8,128)(2,1)} %get-tuple-element.196, f32[196,512]{1,0:T(8,128)S(1)} %get-tuple-element.165, f32[512]{0:T(512)} %get-tuple-element.195, f32[196]{0:T(256)S(1)} %add_rsqrt_fusion.2, f32[196]{0:T(256)S(1)} %broadcast_multiply_fusion.2), kind=kOutput, calls=%fused_computation.5.clone.1 | convolution fusion | flops 308983808 | bytes 2580000 | tf_op jit(solution)/shard_map/while/body/eval_jaxpr/dot_general | solution.py:471
  97.6 0.3 copy.37
  97.9 3.0 %fusion.47 = (f32[16,196]{1,0:T(8,128)S(1)}, f32[16,196,196]{1,2,0:T(8,128)}) fusion(bf16[1,196,3,16,32]{1,4,3,2,0:T(8,128)(2,1)S(1)} %bitcast.88), kind=kOutput, calls=%fused_computation.44.clone.1 | convolution fusion | flops 41182148 | bytes 2995456 | tf_op jit(solution)/shard_map/while/body/eval_jaxpr/sub | solution.py:482
  100.9 2.5 %fusion.48 = bf16[16,32,196]{2,1,0:T(8,128)(2,1)S(1)} fusion(f32[16,196,196]{1,2,0:T(8,128)} %get-tuple-element.167, f32[16,196]{1,0:T(8,128)S(1)} %get-tuple-element.168, bf16[1,196,3,16,32]{1,4,3,2,0:T(8,128)(2,1)S(1)} %bitcast.89), kind=kOutput, calls=%fused_computation.11.clone.1 | convolution fusion | flops 40667648 | bytes 2937856 | tf_op jit(solution)/shard_map/while/body/eval_jaxpr/ihqk,ikhc->iqhc/dot_general | solution.py:484
  103.3 0.3 fusion.49
  103.7 0.1 fusion.45
  103.8 0.7 convert_element_type.63
  104.4 1.3 fusion.46
  105.8 0.2 multiply_reduce_fusion.3
  106.0 2.0 %convolution_convert_fusion.2 = bf16[196,1536]{1,0:T(8,128)(2,1)S(1)} fusion(bf16[512,1536]{1,0:T(8,128)(2,1)} %get-tuple-element.196, f32[196,512]{1,0:T(8,128)S(1)} %get-tuple-element.165, f32[512]{0:T(512)} %get-tuple-element.195, f32[196]{0:T(256)S(1)} %add_rsqrt_fusion.2, f32[196]{0:T(256)S(1)} %broadcast_multiply_fusion.2), kind=kOutput, calls=%fused_computation.5.clone.1 | convolution fusion | flops 308983808 | bytes 2580000 | tf_op jit(solution)/shard_map/while/body/eval_jaxpr/dot_general | solution.py:471
  108.0 0.3 copy.37
  108.3 3.0 %fusion.47 = (f32[16,196]{1,0:T(8,128)S(1)}, f32[16,196,196]{1,2,0:T(8,128)}) fusion(bf16[1,196,3,16,32]{1,4,3,2,0:T(8,128)(2,1)S(1)} %bitcast.88), kind=kOutput, calls=%fused_computation.44.clone.1 | convolution fusion | flops 41182148 | bytes 2995456 | tf_op jit(solution)/shard_map/while/body/eval_jaxpr/sub | solution.py:482
  111.3 2.5 %fusion.48 = bf16[16,32,196]{2,1,0:T(8,128)(2,1)S(1)} fusion(f32[16,196,196]{1,2,0:T(8,128)} %get-tuple-element.167, f32[16,196]{1,0:T(8,128)S(1)} %get-tuple-element.168, bf16[1,196,3,16,32]{1,4,3,2,0:T(8,128)(2,1)S(1)} %bitcast.89), kind=kOutput, calls=%fused_computation.11.clone.1 | convolution fusion | flops 40667648 | bytes 2937856 | tf_op jit(solution)/shard_map/while/body/eval_jaxpr/ihqk,ikhc->iqhc/dot_general | solution.py:484
  113.7 0.3 fusion.49
  114.1 0.1 fusion.45
  114.2 0.7 convert_element_type.63
  114.8 1.3 fusion.46
  116.2 0.2 multiply_reduce_fusion.3
  116.4 2.0 %convolution_convert_fusion.2 = bf16[196,1536]{1,0:T(8,128)(2,1)S(1)} fusion(bf16[512,1536]{1,0:T(8,128)(2,1)} %get-tuple-element.196, f32[196,512]{1,0:T(8,128)S(1)} %get-tuple-element.165, f32[512]{0:T(512)} %get-tuple-element.195, f32[196]{0:T(256)S(1)} %add_rsqrt_fusion.2, f32[196]{0:T(256)S(1)} %broadcast_multiply_fusion.2), kind=kOutput, calls=%fused_computation.5.clone.1 | convolution fusion | flops 308983808 | bytes 2580000 | tf_op jit(solution)/shard_map/while/body/eval_jaxpr/dot_general | solution.py:471
  118.4 0.3 copy.37
  118.7 3.0 %fusion.47 = (f32[16,196]{1,0:T(8,128)S(1)}, f32[16,196,196]{1,2,0:T(8,128)}) fusion(bf16[1,196,3,16,32]{1,4,3,2,0:T(8,128)(2,1)S(1)} %bitcast.88), kind=kOutput, calls=%fused_computation.44.clone.1 | convolution fusion | flops 41182148 | bytes 2995456 | tf_op jit(solution)/shard_map/while/body/eval_jaxpr/sub | solution.py:482
  121.7 2.5 %fusion.48 = bf16[16,32,196]{2,1,0:T(8,128)(2,1)S(1)} fusion(f32[16,196,196]{1,2,0:T(8,128)} %get-tuple-element.167, f32[16,196]{1,0:T(8,128)S(1)} %get-tuple-element.168, bf16[1,196,3,16,32]{1,4,3,2,0:T(8,128)(2,1)S(1)} %bitcast.89), kind=kOutput, calls=%fused_computation.11.clone.1 | convolution fusion | flops 40667648 | bytes 2937856 | tf_op jit(solution)/shard_map/while/body/eval_jaxpr/ihqk,ikhc->iqhc/dot_general | solution.py:484
  124.1 0.3 fusion.49
  124.5 0.1 fusion.45
  124.6 0.7 convert_element_type.63
  125.2 1.3 fusion.46
  126.6 0.2 multiply_reduce_fusion.3
  126.8 2.0 %convolution_convert_fusion.2 = bf16[196,1536]{1,0:T(8,128)(2,1)S(1)} fusion(bf16[512,1536]{1,0:T(8,128)(2,1)} %get-tuple-element.196, f32[196,512]{1,0:T(8,128)S(1)} %get-tuple-element.165, f32[512]{0:T(512)} %get-tuple-element.195, f32[196]{0:T(256)S(1)} %add_rsqrt_fusion.2, f32[196]{0:T(256)S(1)} %broadcast_multiply_fusion.2), kind=kOutput, calls=%fused_computation.5.clone.1 | convolution fusion | flops 308983808 | bytes 2580000 | tf_op jit(solution)/shard_map/while/body/eval_jaxpr/dot_general | solution.py:471
  128.8 0.3 copy.37
  129.1 3.0 %fusion.47 = (f32[16,196]{1,0:T(8,128)S(1)}, f32[16,196,196]{1,2,0:T(8,128)}) fusion(bf16[1,196,3,16,32]{1,4,3,2,0:T(8,128)(2,1)S(1)} %bitcast.88), kind=kOutput, calls=%fused_computation.44.clone.1 | convolution fusion | flops 41182148 | bytes 2995456 | tf_op jit(solution)/shard_map/while/body/eval_jaxpr/sub | solution.py:482
  132.1 2.5 %fusion.48 = bf16[16,32,196]{2,1,0:T(8,128)(2,1)S(1)} fusion(f32[16,196,196]{1,2,0:T(8,128)} %get-tuple-element.167, f32[16,196]{1,0:T(8,128)S(1)} %get-tuple-element.168, bf16[1,196,3,16,32]{1,4,3,2,0:T(8,128)(2,1)S(1)} %bitcast.89), kind=kOutput, calls=%fused_computation.11.clone.1 | convolution fusion | flops 40667648 | bytes 2937856 | tf_op jit(solution)/shard_map/while/body/eval_jaxpr/ihqk,ikhc->iqhc/dot_general | solution.py:484
  134.5 0.3 fusion.49
  134.8 1.3 copy.35
  (32 shorter events, 0.3 us)
Async XLA Ops:
  2.2 1.2 copy-start
  3.4 1.0 copy-start.1
  4.4 0.9 copy-start.2
  5.3 0.9 copy-start.3
  6.2 0.7 copy-start.4
  6.9 0.7 copy-start.5
  100.9 2.5 %copy-start.6 = (bf16[512,512]{1,0:T(8,128)(2,1)S(1)}, bf16[512,512]{1,0:T(8,128)(2,1)}, u32[]{:S(2)}) copy-start(bf16[512,512]{1,0:T(8,128)(2,1)} %get-tuple-element.197) | copy-start | bytes 1572868 | tf_op jit(solution)/shard_map/while
  111.3 2.5 %copy-start.6 = (bf16[512,512]{1,0:T(8,128)(2,1)S(1)}, bf16[512,512]{1,0:T(8,128)(2,1)}, u32[]{:S(2)}) copy-start(bf16[512,512]{1,0:T(8,128)(2,1)} %get-tuple-element.197) | copy-start | bytes 1572868 | tf_op jit(solution)/shard_map/while
  121.7 2.5 %copy-start.6 = (bf16[512,512]{1,0:T(8,128)(2,1)S(1)}, bf16[512,512]{1,0:T(8,128)(2,1)}, u32[]{:S(2)}) copy-start(bf16[512,512]{1,0:T(8,128)(2,1)} %get-tuple-element.197) | copy-start | bytes 1572868 | tf_op jit(solution)/shard_map/while
  132.1 2.5 %copy-start.6 = (bf16[512,512]{1,0:T(8,128)(2,1)S(1)}, bf16[512,512]{1,0:T(8,128)(2,1)}, u32[]{:S(2)}) copy-start(bf16[512,512]{1,0:T(8,128)(2,1)} %get-tuple-element.197) | copy-start | bytes 1572868 | tf_op jit(solution)/shard_map/while

commit v2 on v1

--- a/solution.py
+++ b/solution.py
@@ -25,6 +25,9 @@
 PART = 48
 EPSILON = 1e-06
 TOKENS_AT = 20.0
+IMAGES = 4
+KEYS = 256
+QUERIES = 208
 
 
 def layer_norm(values, factor):
@@ -130,16 +133,23 @@
 
 
 def expert_kernel(
-    tokens_ref,
+    tokens_hbm,
     weight_ref,
-    meta_ref,
-    gain_ref,
+    ids_ref,
+    visible_ref,
+    owner_ref,
+    gain_hbm,
     in_ref,
     out_ref,
+    final_hbm,
+    embed_hbm,
+    rows_ref,
+    own_meta_ref,
+    tokens_ref,
+    gain_ref,
     final_ref,
     embed_ref,
-    rows_ref,
-    own_meta_ref,
+    meta_ref,
     w,
     tokens_pad,
     send,
@@ -176,6 +186,19 @@
     )
     own_in.start()
     own_out.start()
+    fetches = [
+        pltpu.make_async_copy(src, dst, local_sems.at[2 + n])
+        for n, (src, dst) in enumerate(
+            (
+                (tokens_hbm, tokens_ref),
+                (gain_hbm, gain_ref),
+                (final_hbm, final_ref),
+                (embed_hbm, embed_ref),
+            )
+        )
+    ]
+    for fetch in fetches:
+        fetch.start()
     barrier = pltpu.get_barrier_semaphore()
     for near in (
         at_z(0) * NX + at_x(1),
@@ -195,6 +218,14 @@
         )
     got[:, CAP:SLOT, :] = jnp.zeros((EXPERTS, SLOT - CAP, WIDE), jnp.bfloat16)
     back[:, CAP:SLOT, :] = jnp.zeros((EXPERTS, SLOT - CAP, DD), jnp.bfloat16)
+    pad = jnp.full((1, 256 - TOK), -1, jnp.int32)
+    meta_ref[0:1, :] = jnp.concatenate([ids_ref[...], pad], axis=1)
+    for i in range(IMAGES):
+        parts = [visible_ref[i : i + 1, :], jnp.full((1, 256 - VIS * (i + 1)), -1, jnp.int32)]
+        if i > 0:
+            parts = [jnp.full((1, VIS * i), -1, jnp.int32)] + parts
+        meta_ref[i + 1 : i + 2, :] = jnp.concatenate(parts, axis=1)
+    meta_ref[5:8, :] = jnp.full((3, 256), owner_ref[0], jnp.int32)
     own_in.wait()
     own_out.wait()
     pl.semaphore_wait(barrier, 4 + EXPERTS - 1)
@@ -268,10 +299,15 @@
         meta_copy(d, True).start()
     metas[me] = meta_ref[...]
 
+    for fetch in fetches:
+        fetch.wait()
     tokens_pad[TOK // 8 * 8 :, :] = jnp.zeros((256 - TOK // 8 * 8, D), jnp.bfloat16)
     tokens_pad[0:TOK, :] = tokens_ref[...]
     placing = slots_of(meta_ref[0:1, :], ROWS)
-    scale = jnp.sum(placing * weight_ref[...], axis=1, keepdims=True)
+    weight_row = jnp.concatenate(
+        [weight_ref[...].astype(jnp.float32), jnp.zeros((1, 256 - TOK), jnp.float32)], axis=1
+    )
+    scale = jnp.sum(placing * weight_row, axis=1, keepdims=True)
     picked = jnp.dot(
         placing.astype(jnp.bfloat16), tokens_pad[...], preferred_element_type=jnp.float32
     ).astype(jnp.bfloat16)
@@ -373,7 +409,8 @@
 
 def expert_stage(*operands):
     vmem = pl.BlockSpec(memory_space=pltpu.VMEM)
-    hbm = pl.BlockSpec(memory_space=pl.ANY)
+    hbm = pl.BlockSpec(memory_space=pltpu.HBM)
+    smem = pl.BlockSpec(memory_space=pltpu.SMEM)
     count = len(build_plan()[3])
     dma = pltpu.SemaphoreType.DMA
     return pl.pallas_call(
@@ -382,9 +419,14 @@
             jax.ShapeDtypeStruct((256, DD), jnp.bfloat16),
             jax.ShapeDtypeStruct((8, 256), jnp.int32),
         ),
-        in_specs=[vmem, vmem, vmem, vmem, hbm, hbm, vmem, vmem],
+        in_specs=[hbm, vmem, vmem, vmem, smem, hbm, hbm, hbm, hbm, hbm],
         out_specs=(vmem, vmem),
         scratch_shapes=[
+            pltpu.VMEM((TOK, D), jnp.bfloat16),
+            pltpu.VMEM((1, D), jnp.float32),
+            pltpu.VMEM((1, D), jnp.float32),
+            pltpu.VMEM((D, DD), jnp.bfloat16),
+            pltpu.VMEM((8, 256), jnp.int32),
             pltpu.VMEM((NZ, NX, 2 * UNITS, D), jnp.bfloat16),
             pltpu.VMEM((256, D), jnp.bfloat16),
             pltpu.VMEM((EXPERTS, SLOT, WIDE), jnp.bfloat16),
@@ -394,7 +436,7 @@
             pltpu.VMEM((ROWS, D), jnp.float32),
             pltpu.VMEM((EXPERTS, SLOT, DD), jnp.bfloat16),
             pltpu.VMEM((EXPERTS, SLOT, DD), jnp.bfloat16),
-            dma((2,)),
+            dma((6,)),
             dma((count,)),
             dma((count,)),
             dma((EXPERTS,)),
@@ -405,8 +447,77 @@
             dma((EXPERTS,)),
         ],
         compiler_params=pltpu.CompilerParams(
-            collective_id=0, has_side_effects=True, vmem_limit_bytes=48 * 1024 * 1024
+            collective_id=0, has_side_effects=True, vmem_limit_bytes=67043328
         ),
+    )(*operands)
+
+
+def decoder_kernel(
+    rows_ref, meta_ref, mask_ref, pos_ref, gain_ref, in_ref, out_w_ref, out_ref, start, projected, mixed
+):
+    start[:, GRID // 8 * 8 :, :] = jnp.zeros((IMAGES, KEYS - GRID // 8 * 8, DD), jnp.float32)
+    mask_row = mask_ref[...].astype(jnp.float32)
+    position = lax.broadcasted_iota(jnp.int32, (GRID, 256), 0)
+
+    @pl.loop(0, IMAGES)
+    def _(i):
+        hit = (position == meta_ref[pl.ds(i + 1, 1), :]).astype(jnp.float32)
+        covered = jnp.sum(hit, axis=1, keepdims=True)
+        placed = jnp.dot(
+            hit.astype(jnp.bfloat16), rows_ref[...], preferred_element_type=jnp.float32
+        )
+        initial = jnp.where(covered > 0.5, placed, mask_row) + pos_ref[...].astype(jnp.float32)
+        start[i, 0:GRID, :] = initial
+        dec_normed = layer_norm(start[i], gain_ref[...]).astype(jnp.bfloat16)
+        projected[i] = jnp.dot(
+            dec_normed, in_ref[...], preferred_element_type=jnp.float32
+        ).astype(jnp.bfloat16)
+
+    lane = lax.broadcasted_iota(jnp.int32, (QUERIES, KEYS), 1)
+    head_lane = lax.div(lax.broadcasted_iota(jnp.int32, (1, 128), 1), HEAD_DIM)
+    own_lanes = [(head_lane == h).astype(jnp.float32).astype(jnp.bfloat16) for h in range(4)]
+    exponent = HEAD_DIM ** (-0.5) * 1.4426950408889634
+
+    @pl.loop(0, IMAGES)
+    def _(i):
+        for g in range(HEADS // 4):
+            queries = projected[i, 0:QUERIES, g * 128 : (g + 1) * 128]
+            keys = projected[i, :, DD + g * 128 : DD + (g + 1) * 128]
+            values = projected[i, :, 2 * DD + g * 128 : 2 * DD + (g + 1) * 128]
+            total = jnp.zeros((QUERIES, 128), jnp.float32)
+            for h in range(4):
+                scores = lax.dot_general(
+                    queries,
+                    keys * own_lanes[h],
+                    (((1,), (1,)), ((), ())),
+                    preferred_element_type=jnp.float32,
+                )
+                scores = jnp.where(lane < GRID, scores, -jnp.inf)
+                highest = jnp.max(scores, axis=1, keepdims=True)
+                raised = jnp.exp2((scores - highest) * exponent)
+                share = 1.0 / jnp.sum(raised, axis=1, keepdims=True)
+                weights = (raised * share).astype(jnp.bfloat16)
+                total = total + jnp.dot(
+                    weights, values * own_lanes[h], preferred_element_type=jnp.float32
+                )
+            mixed[:, g * 128 : (g + 1) * 128] = total.astype(jnp.bfloat16)
+        update = jnp.dot(mixed[...], out_w_ref[...], preferred_element_type=jnp.float32)
+        out_ref[i] = (start[i, 0:GRID, :] + update[0:GRID]).astype(jnp.bfloat16)
+
+
+def decoder_stage(*operands):
+    vmem = pl.BlockSpec(memory_space=pltpu.VMEM)
+    return pl.pallas_call(
+        decoder_kernel,
+        out_shape=jax.ShapeDtypeStruct((IMAGES, GRID, DD), jnp.bfloat16),
+        in_specs=[vmem] * 7,
+        out_specs=vmem,
+        scratch_shapes=[
+            pltpu.VMEM((IMAGES, KEYS, DD), jnp.float32),
+            pltpu.VMEM((IMAGES, KEYS, 3 * DD), jnp.bfloat16),
+            pltpu.VMEM((QUERIES, DD), jnp.bfloat16),
+        ],
+        compiler_params=pltpu.CompilerParams(vmem_limit_bytes=67043328),
     )(*operands)
 
 
@@ -427,70 +538,27 @@
     attention_in,
     attention_out,
 ):
-    img_dev = visible.shape[0]
-    meta = jnp.concatenate(
-        [
-            jnp.pad(expert_ids.reshape(1, TOK), ((0, 0), (0, 256 - TOK)), constant_values=-1),
-            jnp.pad(visible, ((0, 0), (0, 256 - VIS))),
-            jnp.broadcast_to(owner_map[0], (3, 256)),
-        ],
-        axis=0,
-    )
-    weight_row = jnp.pad(
-        route_weight.astype(jnp.float32).reshape(1, TOK), ((0, 0), (0, 256 - TOK))
-    )
     embedded, own_meta = expert_stage(
         tokens,
-        weight_row,
-        meta,
+        route_weight.reshape(1, TOK),
+        expert_ids.reshape(1, TOK),
+        visible,
+        owner_map,
         norm_gain.reshape(1, D),
         expert_in,
         expert_out,
         final_gain.reshape(1, D),
         embed_weight,
     )
-    source_visible = own_meta[1:5, 0:VIS]
-    image_rows = embedded[0:TOK].reshape(img_dev, 1, VIS, DD)
-    image_places = source_visible.reshape(img_dev, 1, VIS)
-
-    def decode_image(operands):
-        rows_one, places_one = operands
-        position_hit = places_one[:, :, None] == jnp.arange(GRID, dtype=jnp.int32)[None, None, :]
-        covered = jnp.any(position_hit, axis=1)
-        placed = jnp.einsum(
-            "ivg,ivd->igd",
-            position_hit.astype(jnp.bfloat16),
-            rows_one,
-            preferred_element_type=jnp.float32,
-        )
-        canvas = jnp.where(
-            covered[:, :, None], placed, mask_token.astype(jnp.float32)[None, None, :]
-        )
-        initial = canvas + decoder_pos.astype(jnp.float32)[None]
-        dec_normed = layer_norm(initial, decoder_gain).astype(jnp.bfloat16)
-        projected = jnp.dot(
-            dec_normed.reshape(GRID, DD), attention_in, preferred_element_type=jnp.float32
-        ).astype(jnp.bfloat16)
-        projected = projected.reshape(1, GRID, 3, HEADS, HEAD_DIM)
-        queries = projected[:, :, 0]
-        key_rows = projected[:, :, 1]
-        value_rows = projected[:, :, 2]
-        scores = jnp.einsum(
-            "iqhc,ikhc->ihqk", queries, key_rows, preferred_element_type=jnp.float32
-        ) * HEAD_DIM ** (-0.5)
-        highest = jnp.max(scores, axis=-1, keepdims=True)
-        raised = jnp.exp(scores - highest)
-        weights = (raised / jnp.sum(raised, axis=-1, keepdims=True)).astype(jnp.bfloat16)
-        mixed = jnp.einsum(
-            "ihqk,ikhc->iqhc", weights, value_rows, preferred_element_type=jnp.float32
-        ).astype(jnp.bfloat16)
-        update_out = jnp.dot(
-            mixed.reshape(GRID, DD), attention_out, preferred_element_type=jnp.float32
-        )
-        return (initial + update_out.reshape(1, GRID, DD)).astype(jnp.bfloat16)
-
-    decoded = lax.map(decode_image, (image_rows, image_places))
-    return decoded.reshape(img_dev, GRID, DD)
+    return decoder_stage(
+        embedded,
+        own_meta,
+        mask_token.reshape(1, DD),
+        decoder_pos,
+        decoder_gain.reshape(1, DD),
+        attention_in,
+        attention_out,
+    )
 
 
 def solution(mesh):

time: 137 us -> 113 us (0.82)
  matrix products: 36.3 us -> 0 us
  Pallas kernels: 85.5 us -> 108 us
  other arithmetic: 4.74 us -> 0 us
  local copies, waits for them, and re-layouts: 9.29 us -> 4.93 us
    dot_general x16 -> x0, matrix products: 24.3 us -> none  [the longest x4 9.83 us: decode_image(): jnp.einsum('ihqk,ikhc->iqhc', weights, value_rows, preferred_element_type...]
    pallas_call x0 -> x1, Pallas kernels: none -> 21.3 us  [decoder_stage(): pl.pallas_call(decoder_kernel, out_shape=jax.ShapeDtypeStruct((IMAGES, GR...]
    sub x4 -> x0, matrix products: 12 us -> none  [decode_image(): raised = jnp.exp(scores - highest)]
    unnamed x12 -> x0, local copies, waits for them, and re-layouts: 5.41 us -> none
    convert_element_type x4 -> x0, other arithmetic: 2.73 us -> none  [decode_image(): mask_token.astype(jnp.float32)[None, None, :]]
    pallas_call x0 -> x1, local copies, waits for them, and re-layouts: none -> 2.44 us  [decoder_stage(): pl.pallas_call(decoder_kernel, out_shape=jax.ShapeDtypeStruct((IMAGES, GR...]
    reshape x2, local copies, waits for them, and re-layouts: 0.72 us -> 2.49 us  [the longest x1 1.26 us: per_device(): mask_token.reshape(1, DD)]
where the time goes in v2:
time: 113 us
  Pallas kernels  108 us (96%)
  local copies, waits for them, and re-layouts  4.93 us (4%)
    pallas_call x1, Pallas kernels, expert_stage(): pl.pallas_call(expert_kernel, out_shape=(jax.ShapeDtypeStruct((256, DD),...  86.4 us
    pallas_call x1, Pallas kernels, decoder_stage(): pl.pallas_call(decoder_kernel, out_shape=jax.ShapeDtypeStruct((IMAGES, GR...  21.3 us
    pallas_call x1, local copies, waits for them, and re-layouts, decoder_stage(): pl.pallas_call(decoder_kernel, out_shape=jax.ShapeDtypeStruct((IMAGES, GR...  2.44 us

profile of v2, /device:TPU:1, one launch (start us, length us, event | category | flops | bytes accessed | tf_op | source)
XLA Modules:
  0.0 112.6 jit_solution(3407537210050861193)
XLA Ops:
  0.0 1.2 %reshape.18.weight_ref = bf16[1,196]{1,0:T(2,128)(2,1)} reshape(bf16[196]{0:T(256)(128)(2,1)} %param.16) | data formatting | bytes 784 | tf_op jit(solution)/shard_map/reshape | solution.py:543
  1.2 1.3 %reshape.22.mask_ref = bf16[1,512]{1,0:T(2,128)(2,1)} reshape(bf16[512]{0:T(512)(128)(2,1)} %param.25) | data formatting | bytes 2048 | tf_op jit(solution)/shard_map/reshape | solution.py:556
  2.5 86.4 %shard_map.145 = (bf16[256,512]{1,0:T(8,128)(2,1)}, s32[8,256]{1,0:T(8,128)}) custom-call(bf16[196,1024]{1,0:T(8,128)(2,1)} %tokens_hbm.1, bf16[1,196]{1,0:T(2,128)(2,1)} %reshape.18.weight_ref, s32[1,196]{1,0:T(1,128)} %bitcast.7, s32[4,49]{1,0:T(4,128)} %visible_ref.1, s32[4]{0:T(128)} %owner_ref.1, f32[1,1024]{1,0:T(1,128)} %bitcast.4, ...), custom_call_target="tpu_custom_call" | custom-call | tf_op jit(solution)/shard_map/pallas_call | solution.py:416
  88.9 21.3 %shard_map.146 = bf16[4,196,512]{2,1,0:T(8,128)(2,1)} custom-call(bf16[256,512]{1,0:T(8,128)(2,1)} %get-tuple-element.7.rows_ref, s32[8,256]{1,0:T(8,128)} %get-tuple-element.8.meta_ref, bf16[1,512]{1,0:T(2,128)(2,1)} %reshape.22.mask_ref, bf16[196,512]{1,0:T(8,128)(2,1)} %pos_ref.1, f32[1,512]{1,0:T(1,128)} %bitcast.6, bf16[512,1536]{1,0:T(8,128)(2,1)} %in_ref.3, ...), custom_call_target="tpu_custom_call" | custom-call | tf_op jit(solution)/shard_map/pallas_call | solution.py:510
  110.2 2.4 %copy.16 = bf16[4,196,512]{2,0,1:T(4,128)(2,1)} copy(bf16[4,196,512]{2,1,0:T(8,128)(2,1)} %shard_map.146) | data formatting | bytes 1605632 | tf_op jit(solution)/shard_map/pallas_call | solution.py:510

commit v3 on v2

--- a/solution.py
+++ b/solution.py
@@ -26,8 +26,9 @@
 EPSILON = 1e-06
 TOKENS_AT = 20.0
 IMAGES = 4
-KEYS = 256
-QUERIES = 208
+LANES = 256
+KEYS = 208
+FULL = 192
 
 
 def layer_norm(values, factor):
@@ -305,7 +306,7 @@
     tokens_pad[0:TOK, :] = tokens_ref[...]
     placing = slots_of(meta_ref[0:1, :], ROWS)
     weight_row = jnp.concatenate(
-        [weight_ref[...].astype(jnp.float32), jnp.zeros((1, 256 - TOK), jnp.float32)], axis=1
+        [weight_ref[...].astype(jnp.float32).reshape(1, TOK), jnp.zeros((1, 256 - TOK), jnp.float32)], axis=1
     )
     scale = jnp.sum(placing * weight_row, axis=1, keepdims=True)
     picked = jnp.dot(
@@ -453,10 +454,10 @@
 
 
 def decoder_kernel(
-    rows_ref, meta_ref, mask_ref, pos_ref, gain_ref, in_ref, out_w_ref, out_ref, start, projected, mixed
+    rows_ref, meta_ref, mask_ref, pos_ref, gain_ref, in_ref, out_w_ref, out_ref, start, projected, values_t, mixed
 ):
-    start[:, GRID // 8 * 8 :, :] = jnp.zeros((IMAGES, KEYS - GRID // 8 * 8, DD), jnp.float32)
-    mask_row = mask_ref[...].astype(jnp.float32)
+    start[:, GRID // 8 * 8 :, :] = jnp.zeros((IMAGES, LANES - GRID // 8 * 8, DD), jnp.float32)
+    mask_row = mask_ref[...].astype(jnp.float32).reshape(1, DD)
     position = lax.broadcasted_iota(jnp.int32, (GRID, 256), 0)
 
     @pl.loop(0, IMAGES)
@@ -469,39 +470,53 @@
         initial = jnp.where(covered > 0.5, placed, mask_row) + pos_ref[...].astype(jnp.float32)
         start[i, 0:GRID, :] = initial
         dec_normed = layer_norm(start[i], gain_ref[...]).astype(jnp.bfloat16)
-        projected[i] = jnp.dot(
-            dec_normed, in_ref[...], preferred_element_type=jnp.float32
-        ).astype(jnp.bfloat16)
-
-    lane = lax.broadcasted_iota(jnp.int32, (QUERIES, KEYS), 1)
+        product = jnp.dot(dec_normed, in_ref[...], preferred_element_type=jnp.float32)
+        projected[i] = product[:, 0 : 2 * DD].astype(jnp.bfloat16)
+        values_t[i] = jnp.transpose(product[:, 2 * DD :]).astype(jnp.bfloat16)
+
     head_lane = lax.div(lax.broadcasted_iota(jnp.int32, (1, 128), 1), HEAD_DIM)
     own_lanes = [(head_lane == h).astype(jnp.float32).astype(jnp.bfloat16) for h in range(4)]
+    tail = lax.broadcasted_iota(jnp.int32, (KEYS - FULL, LANES), 0) < GRID - FULL
     exponent = HEAD_DIM ** (-0.5) * 1.4426950408889634
 
     @pl.loop(0, IMAGES)
     def _(i):
         for g in range(HEADS // 4):
-            queries = projected[i, 0:QUERIES, g * 128 : (g + 1) * 128]
-            keys = projected[i, :, DD + g * 128 : DD + (g + 1) * 128]
-            values = projected[i, :, 2 * DD + g * 128 : 2 * DD + (g + 1) * 128]
-            total = jnp.zeros((QUERIES, 128), jnp.float32)
+            queries = projected[i, :, g * 128 : (g + 1) * 128]
+            keys = projected[i, 0:KEYS, DD + g * 128 : DD + (g + 1) * 128]
             for h in range(4):
                 scores = lax.dot_general(
+                    keys * own_lanes[h],
                     queries,
-                    keys * own_lanes[h],
                     (((1,), (1,)), ((), ())),
                     preferred_element_type=jnp.float32,
                 )
-                scores = jnp.where(lane < GRID, scores, -jnp.inf)
-                highest = jnp.max(scores, axis=1, keepdims=True)
-                raised = jnp.exp2((scores - highest) * exponent)
-                share = 1.0 / jnp.sum(raised, axis=1, keepdims=True)
-                weights = (raised * share).astype(jnp.bfloat16)
-                total = total + jnp.dot(
-                    weights, values * own_lanes[h], preferred_element_type=jnp.float32
+                last = jnp.where(tail, scores[FULL:], -jnp.inf)
+                highest = jnp.maximum(
+                    jnp.max(scores[:FULL], axis=0, keepdims=True),
+                    jnp.max(last, axis=0, keepdims=True),
                 )
-            mixed[:, g * 128 : (g + 1) * 128] = total.astype(jnp.bfloat16)
-        update = jnp.dot(mixed[...], out_w_ref[...], preferred_element_type=jnp.float32)
+                raised = jnp.exp2((scores[:FULL] - highest) * exponent)
+                raised_last = jnp.exp2((last - highest) * exponent)
+                share = 1.0 / (
+                    jnp.sum(raised, axis=0, keepdims=True)
+                    + jnp.sum(raised_last, axis=0, keepdims=True)
+                )
+                weights = jnp.concatenate(
+                    [(raised * share).astype(jnp.bfloat16), (raised_last * share).astype(jnp.bfloat16)],
+                    axis=0,
+                )
+                first = g * 128 + h * HEAD_DIM
+                mixed[first : first + HEAD_DIM, :] = jnp.dot(
+                    values_t[i, first : first + HEAD_DIM, 0:KEYS],
+                    weights,
+                    preferred_element_type=jnp.float32,
+                )
+        update = jnp.dot(
+            jnp.transpose(mixed[...]).astype(jnp.bfloat16),
+            out_w_ref[...],
+            preferred_element_type=jnp.float32,
+        )
         out_ref[i] = (start[i, 0:GRID, :] + update[0:GRID]).astype(jnp.bfloat16)
 
 
@@ -513,9 +528,10 @@
         in_specs=[vmem] * 7,
         out_specs=vmem,
         scratch_shapes=[
-            pltpu.VMEM((IMAGES, KEYS, DD), jnp.float32),
-            pltpu.VMEM((IMAGES, KEYS, 3 * DD), jnp.bfloat16),
-            pltpu.VMEM((QUERIES, DD), jnp.bfloat16),
+            pltpu.VMEM((IMAGES, LANES, DD), jnp.float32),
+            pltpu.VMEM((IMAGES, LANES, 2 * DD), jnp.bfloat16),
+            pltpu.VMEM((IMAGES, DD, LANES), jnp.bfloat16),
+            pltpu.VMEM((DD, LANES), jnp.float32),
         ],
         compiler_params=pltpu.CompilerParams(vmem_limit_bytes=67043328),
     )(*operands)
@@ -540,7 +556,7 @@
 ):
     embedded, own_meta = expert_stage(
         tokens,
-        route_weight.reshape(1, TOK),
+        route_weight,
         expert_ids.reshape(1, TOK),
         visible,
         owner_map,
@@ -553,7 +569,7 @@
     return decoder_stage(
         embedded,
         own_meta,
-        mask_token.reshape(1, DD),
+        mask_token,
         decoder_pos,
         decoder_gain.reshape(1, DD),
         attention_in,

time: 113 us -> 110 us (0.973)
  local copies, waits for them, and re-layouts: 4.93 us -> 2.44 us
    reshape x2 -> x0, local copies, waits for them, and re-layouts: 2.49 us -> none  [the longest x1 1.26 us: per_device(): mask_token.reshape(1, DD)]
where the time goes in v3:
time: 110 us
  Pallas kernels  107 us (97%)
  local copies, waits for them, and re-layouts  2.44 us (2%)
    pallas_call x1, Pallas kernels, expert_stage(): pl.pallas_call(expert_kernel, out_shape=(jax.ShapeDtypeStruct((256, DD),...  86.4 us
    pallas_call x1, Pallas kernels, decoder_stage(): pl.pallas_call(decoder_kernel, out_shape=jax.ShapeDtypeStruct((IMAGES, GR...  20.8 us
    pallas_call x1, local copies, waits for them, and re-layouts, decoder_stage(): pl.pallas_call(decoder_kernel, out_shape=jax.ShapeDtypeStruct((IMAGES, GR...  2.44 us

profile of v3, /device:TPU:1, one launch (start us, length us, event | category | flops | bytes accessed | tf_op | source)
XLA Modules:
  0.0 109.7 jit_solution(2032760514285804809)
XLA Ops:
  0.0 86.4 %shard_map.145 = (bf16[256,512]{1,0:T(8,128)(2,1)}, s32[8,256]{1,0:T(8,128)}) custom-call(bf16[196,1024]{1,0:T(8,128)(2,1)} %tokens_hbm.1, bf16[196]{0:T(256)(128)(2,1)} %weight_ref.1, s32[1,196]{1,0:T(1,128)} %bitcast.7, s32[4,49]{1,0:T(4,128)} %visible_ref.1, s32[4]{0:T(128)} %owner_ref.1, f32[1,1024]{1,0:T(1,128)} %bitcast.4, ...), custom_call_target="tpu_custom_call" | custom-call | tf_op jit(solution)/shard_map/pallas_call | solution.py:417
  86.4 20.8 %shard_map.146 = bf16[4,196,512]{2,1,0:T(8,128)(2,1)} custom-call(bf16[256,512]{1,0:T(8,128)(2,1)} %get-tuple-element.7.rows_ref, s32[8,256]{1,0:T(8,128)} %get-tuple-element.8.meta_ref, bf16[512]{0:T(512)(128)(2,1)} %mask_ref.1, bf16[196,512]{1,0:T(8,128)(2,1)} %pos_ref.1, f32[1,512]{1,0:T(1,128)} %bitcast.6, bf16[512,1536]{1,0:T(8,128)(2,1)} %in_ref.3, ...), custom_call_target="tpu_custom_call" | custom-call | tf_op jit(solution)/shard_map/pallas_call | solution.py:525
  107.2 2.4 %copy.16 = bf16[4,196,512]{2,0,1:T(4,128)(2,1)} copy(bf16[4,196,512]{2,1,0:T(8,128)(2,1)} %shard_map.146) | data formatting | bytes 1605632 | tf_op jit(solution)/shard_map/pallas_call | solution.py:525

commit v4 on v3

--- a/solution.py
+++ b/solution.py
@@ -151,6 +151,8 @@
     final_ref,
     embed_ref,
     meta_ref,
+    permute_ref,
+    table_ref,
     w,
     tokens_pad,
     send,
@@ -320,6 +322,26 @@
         token_copy(d, True).start()
     got[me, 0:CAP, :] = send[me, 0:CAP, :]
 
+    def route_back():
+        for d in range(1, EXPERTS):
+            meta_copy(d, False).wait_recv()
+        owners = metas[:, 5, :][:, 0:1]
+        lane = lax.broadcasted_iota(jnp.int32, (EXPERTS, ROWS), 1)
+        member = lax.broadcasted_iota(jnp.int32, (EXPERTS, ROWS), 0)
+        owner_lane = jnp.sum(
+            jnp.where(lax.div(lane, SLOT) == member, owners, 0), axis=0, keepdims=True
+        )
+        row_at = lax.broadcasted_iota(jnp.int32, (ROWS, ROWS), 0)
+        lane_at = lax.broadcasted_iota(jnp.int32, (ROWS, ROWS), 1)
+        target_row = owner_lane * SLOT + lax.rem(lane_at[0:1, :], SLOT)
+        permute_ref[...] = (row_at == target_row).astype(jnp.float32).astype(jnp.bfloat16)
+        own_meta = jnp.zeros((8, 256), jnp.int32)
+        for s in range(EXPERTS):
+            entry = metas[s]
+            own_meta = own_meta + jnp.where(entry[5:6, :] == me, entry, 0)
+        own_meta_ref[...] = own_meta
+        table_ref[...] = jnp.transpose(slots_of(own_meta[0:1, :], ROWS)).astype(jnp.bfloat16)
+
     def begin_tokens():
         for d in range(1, EXPERTS):
             token_copy(d, False).wait_recv()
@@ -355,6 +377,7 @@
         arrived.add(copy)
         if not begun and now > TOKENS_AT:
             begin_tokens()
+            route_back()
             begun = True
         if begun:
             for k in range(NZ):
@@ -369,36 +392,18 @@
     embedded = jnp.dot(
         final_normed, embed_ref[...], preferred_element_type=jnp.float32
     ).astype(jnp.bfloat16)
-    for d in range(1, EXPERTS):
-        meta_copy(d, False).wait_recv()
-    owners = metas[:, 5, :][:, 0:1]
-    lane = lax.broadcasted_iota(jnp.int32, (EXPERTS, ROWS), 1)
-    member = lax.broadcasted_iota(jnp.int32, (EXPERTS, ROWS), 0)
-    owner_lane = jnp.sum(
-        jnp.where(lax.div(lane, SLOT) == member, owners, 0), axis=0, keepdims=True
-    )
-    row_at = lax.broadcasted_iota(jnp.int32, (ROWS, ROWS), 0)
-    lane_at = lax.broadcasted_iota(jnp.int32, (ROWS, ROWS), 1)
-    target_row = owner_lane * SLOT + lax.rem(lane_at[0:1, :], SLOT)
-    permute = (row_at == target_row).astype(jnp.float32).astype(jnp.bfloat16)
     outgoing[...] = (
-        jnp.dot(permute, embedded, preferred_element_type=jnp.float32)
+        jnp.dot(permute_ref[...], embedded, preferred_element_type=jnp.float32)
         .astype(jnp.bfloat16)
         .reshape(EXPERTS, SLOT, DD)
     )
     for d in range(1, EXPERTS):
         back_copy(d, True).start()
     back[me, 0:CAP, :] = outgoing[me, 0:CAP, :]
-    own_meta = jnp.zeros((8, 256), jnp.int32)
-    for s in range(EXPERTS):
-        entry = metas[s]
-        own_meta = own_meta + jnp.where(entry[5:6, :] == me, entry, 0)
-    own_meta_ref[...] = own_meta
-    table = jnp.transpose(slots_of(own_meta[0:1, :], ROWS)).astype(jnp.bfloat16)
     for d in range(1, EXPERTS):
         back_copy(d, False).wait_recv()
     rows_ref[...] = jnp.dot(
-        table, back[...].reshape(ROWS, DD), preferred_element_type=jnp.float32
+        table_ref[...], back[...].reshape(ROWS, DD), preferred_element_type=jnp.float32
     ).astype(jnp.bfloat16)
     for copy in ids:
         weight_copy(copy, False).wait_send()
@@ -428,6 +433,8 @@
             pltpu.VMEM((1, D), jnp.float32),
             pltpu.VMEM((D, DD), jnp.bfloat16),
             pltpu.VMEM((8, 256), jnp.int32),
+            pltpu.VMEM((ROWS, ROWS), jnp.bfloat16),
+            pltpu.VMEM((256, ROWS), jnp.bfloat16),
             pltpu.VMEM((NZ, NX, 2 * UNITS, D), jnp.bfloat16),
             pltpu.VMEM((256, D), jnp.bfloat16),
             pltpu.VMEM((EXPERTS, SLOT, WIDE), jnp.bfloat16),
@@ -457,6 +464,7 @@
     rows_ref, meta_ref, mask_ref, pos_ref, gain_ref, in_ref, out_w_ref, out_ref, start, projected, values_t, mixed
 ):
     start[:, GRID // 8 * 8 :, :] = jnp.zeros((IMAGES, LANES - GRID // 8 * 8, DD), jnp.float32)
+    exponent = HEAD_DIM ** (-0.5) * 1.4426950408889634
     mask_row = mask_ref[...].astype(jnp.float32).reshape(1, DD)
     position = lax.broadcasted_iota(jnp.int32, (GRID, 256), 0)
 
@@ -471,13 +479,13 @@
         start[i, 0:GRID, :] = initial
         dec_normed = layer_norm(start[i], gain_ref[...]).astype(jnp.bfloat16)
         product = jnp.dot(dec_normed, in_ref[...], preferred_element_type=jnp.float32)
-        projected[i] = product[:, 0 : 2 * DD].astype(jnp.bfloat16)
+        projected[i, :, 0:DD] = (product[:, 0:DD] * exponent).astype(jnp.bfloat16)
+        projected[i, :, DD : 2 * DD] = product[:, DD : 2 * DD].astype(jnp.bfloat16)
         values_t[i] = jnp.transpose(product[:, 2 * DD :]).astype(jnp.bfloat16)
 
     head_lane = lax.div(lax.broadcasted_iota(jnp.int32, (1, 128), 1), HEAD_DIM)
     own_lanes = [(head_lane == h).astype(jnp.float32).astype(jnp.bfloat16) for h in range(4)]
     tail = lax.broadcasted_iota(jnp.int32, (KEYS - FULL, LANES), 0) < GRID - FULL
-    exponent = HEAD_DIM ** (-0.5) * 1.4426950408889634
 
     @pl.loop(0, IMAGES)
     def _(i):
@@ -496,22 +504,23 @@
                     jnp.max(scores[:FULL], axis=0, keepdims=True),
                     jnp.max(last, axis=0, keepdims=True),
                 )
-                raised = jnp.exp2((scores[:FULL] - highest) * exponent)
-                raised_last = jnp.exp2((last - highest) * exponent)
+                raised = jnp.exp2(scores[:FULL] - highest)
+                raised_last = jnp.exp2(last - highest)
                 share = 1.0 / (
                     jnp.sum(raised, axis=0, keepdims=True)
                     + jnp.sum(raised_last, axis=0, keepdims=True)
                 )
                 weights = jnp.concatenate(
-                    [(raised * share).astype(jnp.bfloat16), (raised_last * share).astype(jnp.bfloat16)],
+                    [raised.astype(jnp.bfloat16), raised_last.astype(jnp.bfloat16)],
                     axis=0,
                 )
                 first = g * 128 + h * HEAD_DIM
-                mixed[first : first + HEAD_DIM, :] = jnp.dot(
+                summed = jnp.dot(
                     values_t[i, first : first + HEAD_DIM, 0:KEYS],
                     weights,
                     preferred_element_type=jnp.float32,
                 )
+                mixed[first : first + HEAD_DIM, :] = summed * share
         update = jnp.dot(
             jnp.transpose(mixed[...]).astype(jnp.bfloat16),
             out_w_ref[...],

time: 110 us -> 109 us (level)
    pallas_call x1, Pallas kernels: 20.8 us -> 18.6 us  [decoder_stage(): pl.pallas_call(decoder_kernel, out_shape=jax.ShapeDtypeStruct((IMAGES, GR...]
where the time goes in v4:
time: 109 us; the launch traced here: 108 us
  Pallas kernels  106 us (97%)
  local copies, waits for them, and re-layouts  2.44 us (2%)
    pallas_call x1, Pallas kernels, expert_stage(): pl.pallas_call(expert_kernel, out_shape=(jax.ShapeDtypeStruct((256, DD),...  87.4 us
    pallas_call x1, Pallas kernels, decoder_stage(): pl.pallas_call(decoder_kernel, out_shape=jax.ShapeDtypeStruct((IMAGES, GR...  18.6 us
    pallas_call x1, local copies, waits for them, and re-layouts, decoder_stage(): pl.pallas_call(decoder_kernel, out_shape=jax.ShapeDtypeStruct((IMAGES, GR...  2.44 us

profile of v4, /device:TPU:1, one launch (start us, length us, event | category | flops | bytes accessed | tf_op | source)
XLA Modules:
  0.0 108.5 jit_solution(7169444198508313315)
XLA Ops:
  0.0 87.4 %shard_map.145 = (bf16[256,512]{1,0:T(8,128)(2,1)}, s32[8,256]{1,0:T(8,128)}) custom-call(bf16[196,1024]{1,0:T(8,128)(2,1)} %tokens_hbm.1, bf16[196]{0:T(256)(128)(2,1)} %weight_ref.1, s32[1,196]{1,0:T(1,128)} %bitcast.7, s32[4,49]{1,0:T(4,128)} %visible_ref.1, s32[4]{0:T(128)} %owner_ref.1, f32[1,1024]{1,0:T(1,128)} %bitcast.4, ...), custom_call_target="tpu_custom_call" | custom-call | tf_op jit(solution)/shard_map/pallas_call | solution.py:422
  87.4 18.6 %shard_map.146 = bf16[4,196,512]{2,1,0:T(8,128)(2,1)} custom-call(bf16[256,512]{1,0:T(8,128)(2,1)} %get-tuple-element.7.rows_ref, s32[8,256]{1,0:T(8,128)} %get-tuple-element.8.meta_ref, bf16[512]{0:T(512)(128)(2,1)} %mask_ref.1, bf16[196,512]{1,0:T(8,128)(2,1)} %pos_ref.1, f32[1,512]{1,0:T(1,128)} %bitcast.6, bf16[512,1536]{1,0:T(8,128)(2,1)} %in_ref.3, ...), custom_call_target="tpu_custom_call" | custom-call | tf_op jit(solution)/shard_map/pallas_call | solution.py:534
  106.1 2.4 %copy.16 = bf16[4,196,512]{2,0,1:T(4,128)(2,1)} copy(bf16[4,196,512]{2,1,0:T(8,128)(2,1)} %shard_map.146) | data formatting | bytes 1605632 | tf_op jit(solution)/shard_map/pallas_call | solution.py:534

commit v5 on v4

--- a/solution.py
+++ b/solution.py
@@ -24,7 +24,7 @@
 UNITS = 64
 PART = 48
 EPSILON = 1e-06
-TOKENS_AT = 20.0
+TOKENS_AT = 26.0
 IMAGES = 4
 LANES = 256
 KEYS = 208
@@ -50,7 +50,11 @@
     return 2 if (way == 1) == (k % 2 == 0) else 1
 
 
-def a_from(j):
+def gate(j):
+    return ("b1", 1, {0: 1, 1: 2, 2: 3, 3: 2}[j])
+
+
+def has_rows(j):
     return {0: None, 1: ("a1", 0), 2: ("a1", 2), 3: ("a1", 1)}[j]
 
 
@@ -72,7 +76,7 @@
     for j in range(NX):
         for way in (1, -1):
             for t in range(1, a2_max(j, way) + 1):
-                need[("a2", j, way, t)] = a_from(j) if t == 1 else ("a2", j, way, t - 1)
+                need[("a2", j, way, t)] = gate(j) if t == 1 else ("a2", j, way, t - 1)
 
     def link(copy):
         if copy[0] == "a1":
@@ -98,7 +102,9 @@
         now, _, copy = heapq.heappop(arrivals)
         nexts = [c for c in need if need[c] == copy]
         order.append((now, copy, nexts))
+        seen = [entry[1] for entry in order]
         for c in nexts:
+            assert c[0] != "a2" or has_rows(c[1]) is None or has_rows(c[1]) in seen
             push(c, now)
     slabs = []
     for k in range(NZ):

time: 109 us -> 104 us (0.954)
  Pallas kernels: 106 us -> 101 us
    pallas_call x1, Pallas kernels: 87.4 us -> 82.9 us  [expert_stage(): pl.pallas_call(expert_kernel, out_shape=(jax.ShapeDtypeStruct((256, DD),...]
where the time goes in v5:
time: 104 us
  Pallas kernels  101 us (97%)
  local copies, waits for them, and re-layouts  2.44 us (2%)
    pallas_call x1, Pallas kernels, expert_stage(): pl.pallas_call(expert_kernel, out_shape=(jax.ShapeDtypeStruct((256, DD),...  82.9 us
    pallas_call x1, Pallas kernels, decoder_stage(): pl.pallas_call(decoder_kernel, out_shape=jax.ShapeDtypeStruct((IMAGES, GR...  18.6 us
    pallas_call x1, local copies, waits for them, and re-layouts, decoder_stage(): pl.pallas_call(decoder_kernel, out_shape=jax.ShapeDtypeStruct((IMAGES, GR...  2.44 us

profile of v5, /device:TPU:1, one launch (start us, length us, event | category | flops | bytes accessed | tf_op | source)
XLA Modules:
  0.0 103.9 jit_solution(9237778078863866872)
XLA Ops:
  0.0 82.9 %shard_map.145 = (bf16[256,512]{1,0:T(8,128)(2,1)}, s32[8,256]{1,0:T(8,128)}) custom-call(bf16[196,1024]{1,0:T(8,128)(2,1)} %tokens_hbm.1, bf16[196]{0:T(256)(128)(2,1)} %weight_ref.1, s32[1,196]{1,0:T(1,128)} %bitcast.7, s32[4,49]{1,0:T(4,128)} %visible_ref.1, s32[4]{0:T(128)} %owner_ref.1, f32[1,1024]{1,0:T(1,128)} %bitcast.4, ...), custom_call_target="tpu_custom_call" | custom-call | tf_op jit(solution)/shard_map/pallas_call | solution.py:428
  82.9 18.6 %shard_map.146 = bf16[4,196,512]{2,1,0:T(8,128)(2,1)} custom-call(bf16[256,512]{1,0:T(8,128)(2,1)} %get-tuple-element.7.rows_ref, s32[8,256]{1,0:T(8,128)} %get-tuple-element.8.meta_ref, bf16[512]{0:T(512)(128)(2,1)} %mask_ref.1, bf16[196,512]{1,0:T(8,128)(2,1)} %pos_ref.1, f32[1,512]{1,0:T(1,128)} %bitcast.6, bf16[512,1536]{1,0:T(8,128)(2,1)} %in_ref.3, ...), custom_call_target="tpu_custom_call" | custom-call | tf_op jit(solution)/shard_map/pallas_call | solution.py:540
  101.5 2.4 %copy.16 = bf16[4,196,512]{2,0,1:T(4,128)(2,1)} copy(bf16[4,196,512]{2,1,0:T(8,128)(2,1)} %shard_map.146) | data formatting | bytes 1605632 | tf_op jit(solution)/shard_map/pallas_call | solution.py:540
